TPU v7x, 32 devices: a whole 2x2x4 slice. The times are simulated.
32 devices in a mesh: dp: 4 (over y, core), tensor: 8 (over z, x).
Axes of the slice: x: 2, y: 2, z: 4, core: 2. Of those that a mesh axis runs over, the one named last changes fastest.
Arguments:
- tokens: bfloat16 [512, 8192], P('dp', 'tensor'), may hold values from -6 to 6
- grad_out: bfloat16 [512, 8192], P('dp', 'tensor'), may hold values from -6 to 6
- packed_weight_blocks: float32 [2048, 128, 128], P(('dp', 'tensor')), may hold values from -4 to 4
- packed_first_moments: float32 [2048, 128, 128], P(('dp', 'tensor')), may hold values from -2 to 2
- packed_second_moments: float32 [2048, 128, 128], P(('dp', 'tensor')), may hold values from 0.05 to 1
- block_mask: int32 [2, 64, 128], P(None, None, 'tensor'), may hold values from 0 to 1, as said below
- last_step: int32 [2, 64, 128], P(None, None, 'tensor'), may hold values from 130 to 139
- regrown: int32 [2, 64, 128], P(None, None, 'tensor'), may hold values 0 or 1
- step_now: int32 [1], replicated, may hold values from 140 to 149
Outputs:
- input_grad: bfloat16 [512, 8192], P('dp', 'tensor')
- new_weights: float32 [2048, 128, 128], P(('dp', 'tensor'))
- new_first: float32 [2048, 128, 128], P(('dp', 'tensor'))
- new_second: float32 [2048, 128, 128], P(('dp', 'tensor'))
Inputs may be any that keep to these rules, and one draw needn't show every extreme that they name: `block_mask`: within one tensor shard's 16 block columns, both matrices together hold between 128 and 256 active blocks; some shard holds exactly 256.
All inputs are finite; a program needn't handle non-finite values. No bound on the sum of `regrown` on one device may be relied on, other than what follows from the above.
Results may differ from a plain program's by a relative error of at most 0.014.
Values may be sent and summed in bfloat16 or wider, within the bound.
A program may use at most 192 MiB of HBM per device.

v0:
```python
import math

import jax
import jax.numpy as jnp
from jax import lax
from jax.sharding import PartitionSpec as P

D = 8192


beta_one = 0.9
beta_two = 0.95
learn_rate = 0.05
decay_rate = 0.1
epsilon = 0.05


def silu_slope(values):
    sigmoid = jax.nn.sigmoid(values)
    return sigmoid * (1.0 + values * (1.0 - sigmoid))


def slot_table(mask_grid, regrown_grid, last_grid, slot_total):
    flags = mask_grid.reshape(-1)
    numbered = jnp.cumsum(flags, dtype=jnp.int32) - 1
    block_total = flags.shape[0]
    matches = (numbered[None, :] == jnp.arange(slot_total, dtype=jnp.int32)[:, None]) & (
        flags[None, :] == 1
    )
    block_index = jnp.sum(
        jnp.where(matches, jnp.arange(block_total, dtype=jnp.int32)[None, :], 0),
        axis=1,
        dtype=jnp.int32,
    )
    slot_regrown = jnp.sum(
        jnp.where(matches, regrown_grid.reshape(-1)[None, :], 0), axis=1, dtype=jnp.int32
    )
    slot_last = jnp.sum(
        jnp.where(matches, last_grid.reshape(-1)[None, :], 0), axis=1, dtype=jnp.int32
    )
    live_count = jnp.sum(flags, dtype=jnp.int32)
    return (numbered, block_index, slot_regrown, slot_last, live_count)


def adam_step(
    weights, first_in, second_in, block_grads, live_slots, slot_regrown, slot_last, step_value
):
    regrown_now = (slot_regrown == 1)[:, None, None]
    skipped = (step_value - slot_last - 1).astype(jnp.float32)[:, None, None]
    base_weight = jnp.where(regrown_now, jnp.float32(0.0), weights)
    kept_first = jnp.where(
        regrown_now, jnp.float32(0.0), first_in * jnp.power(jnp.float32(beta_one), skipped)
    )
    kept_second = jnp.where(
        regrown_now, jnp.float32(0.0), second_in * jnp.power(jnp.float32(beta_two), skipped)
    )
    new_first = beta_one * kept_first + (1.0 - beta_one) * block_grads
    new_second = beta_two * kept_second + (1.0 - beta_two) * block_grads * block_grads
    bias_count = jnp.where(
        regrown_now, jnp.float32(1.0), step_value.astype(jnp.float32) + jnp.zeros_like(skipped)
    )
    first_hat = new_first / (1.0 - jnp.power(jnp.float32(beta_one), bias_count))
    second_hat = new_second / (1.0 - jnp.power(jnp.float32(beta_two), bias_count))
    new_weight = base_weight - learn_rate * (
        first_hat / (jnp.sqrt(second_hat) + epsilon) + decay_rate * base_weight
    )
    keep_slot = live_slots[:, None, None]
    return (
        jnp.where(keep_slot, new_weight, weights),
        jnp.where(keep_slot, new_first, first_in),
        jnp.where(keep_slot, new_second, second_in),
    )


def per_device(
    tokens,
    grad_out,
    packed_weight_blocks,
    packed_first_moments,
    packed_second_moments,
    block_mask,
    last_step,
    regrown,
    step_now,
):
    scale_factor = 3.0 / math.sqrt(D)
    tok_count = tokens.shape[0]
    owned_slots = packed_weight_blocks.shape[0]
    block_size = packed_weight_blocks.shape[1]
    row_blocks = block_mask.shape[1]
    column_blocks = block_mask.shape[2]
    groups = lax.axis_size("dp")
    slot_total = owned_slots * groups
    step_value = step_now[0]
    packed = lax.all_gather(packed_weight_blocks.astype(jnp.bfloat16), "dp", axis=0, tiled=True)
    inputs_full, outgrad_full = (
        lax.all_gather(tokens, "tensor", axis=1, tiled=True),
        lax.all_gather(grad_out, "tensor", axis=1, tiled=True),
    )
    numbered, block_index, slot_regrown, slot_last, live_count = slot_table(
        block_mask, regrown, last_step, slot_total
    )
    usable = (block_mask == 1) & (regrown == 0)
    slot_grid = jnp.maximum(numbered, 0).reshape(block_mask.shape)

    def column_step(accum, column_in):
        column_slots, column_used = column_in
        blocks = jnp.take(packed, column_slots.reshape(-1), axis=0).reshape(
            2, row_blocks, block_size, block_size
        )
        blocks = jnp.where(column_used[:, :, None, None], blocks, jnp.zeros((), jnp.bfloat16))
        dense_col = blocks.reshape(2, row_blocks * block_size, block_size)
        pre_act = scale_factor * jnp.dot(
            inputs_full, dense_col[0], preferred_element_type=jnp.float32
        )
        back_act = scale_factor * jnp.dot(
            outgrad_full, dense_col[1], preferred_element_type=jnp.float32
        )
        hidden = jax.nn.silu(pre_act).astype(jnp.bfloat16)
        hidden_grad = (back_act * silu_slope(pre_act)).astype(jnp.bfloat16)
        return (accum, (hidden_grad, hidden))

    column_inputs = (slot_grid.transpose(2, 0, 1), usable.transpose(2, 0, 1))
    accum_shape = (1, 1)
    accum, column_outs = lax.scan(column_step, jnp.zeros(accum_shape, jnp.float32), column_inputs)
    grad_cols, hidden_cols = column_outs
    left_source = jnp.concatenate(
        [
            inputs_full.reshape(tok_count, row_blocks, block_size),
            outgrad_full.reshape(tok_count, row_blocks, block_size),
        ],
        axis=1,
    )
    right_source = jnp.concatenate([grad_cols, hidden_cols], axis=0).transpose(1, 0, 2)
    matrix_of = block_index // (row_blocks * column_blocks)
    row_of = block_index // column_blocks % row_blocks
    column_of = block_index % column_blocks
    left_rows = jnp.take(left_source, matrix_of * row_blocks + row_of, axis=1)
    right_rows = jnp.take(right_source, matrix_of * column_blocks + column_of, axis=1)
    up_blocks = jnp.take(packed, slot_grid[0].reshape(-1), axis=0).reshape(
        row_blocks, column_blocks, block_size, block_size
    )
    up_blocks = jnp.where(usable[0][:, :, None, None], up_blocks, jnp.zeros((), jnp.bfloat16))
    up_dense = up_blocks.transpose(0, 2, 1, 3).reshape(
        row_blocks * block_size, column_blocks * block_size
    )
    grad_flat = grad_cols.transpose(1, 0, 2).reshape(tok_count, column_blocks * block_size)
    summed_rows = lax.psum_scatter(
        (
            scale_factor
            * lax.dot_general(
                up_dense, grad_flat, (((1,), (1,)), ((), ())), preferred_element_type=jnp.float32
            )
        ).astype(jnp.bfloat16),
        "tensor",
        scatter_dimension=0,
        tiled=True,
    ).astype(jnp.float32)
    input_grad = summed_rows.T.astype(jnp.bfloat16)
    block_grads = lax.psum_scatter(
        (
            scale_factor
            * jnp.einsum("tsi,tsj->sij", left_rows, right_rows, preferred_element_type=jnp.float32)
        ).astype(jnp.bfloat16),
        "dp",
        scatter_dimension=0,
        tiled=True,
    ).astype(jnp.float32)
    owner_first = lax.axis_index("dp") * owned_slots
    mine_regrown = lax.dynamic_slice_in_dim(slot_regrown, owner_first, owned_slots)
    mine_last = lax.dynamic_slice_in_dim(slot_last, owner_first, owned_slots)
    live_slots = owner_first + jnp.arange(owned_slots, dtype=jnp.int32) < live_count
    new_weights, new_first, new_second = adam_step(
        packed_weight_blocks,
        packed_first_moments,
        packed_second_moments,
        block_grads,
        live_slots,
        mine_regrown,
        mine_last,
        step_value,
    )
    return (input_grad, new_weights, new_first, new_second)


def solution(mesh):
    in_specs = (
        P("dp", "tensor"),
        P("dp", "tensor"),
        P(("dp", "tensor"), None, None),
        P(("dp", "tensor"), None, None),
        P(("dp", "tensor"), None, None),
        P(None, None, "tensor"),
        P(None, None, "tensor"),
        P(None, None, "tensor"),
        P(),
    )
    out_specs = (
        P("dp", "tensor"),
        P(("dp", "tensor"), None, None),
        P(("dp", "tensor"), None, None),
        P(("dp", "tensor"), None, None),
    )
    return jax.shard_map(
        per_device, mesh=mesh, in_specs=in_specs, out_specs=out_specs, check_vma=False
    )
```

profile of v0, /device:TPU:0, one launch (start us, length us, event | category | flops | bytes accessed | tf_op | source)
XLA Modules:
  0.0 606.6 jit_solution(7807761156665752457)
XLA Ops:
  16.6 45.9 %all-gather.6.cloned.1.call-done = bf16[128,8192]{0,1:T(8,128)(2,1)} async-done(((bf16[128,1024]{0,1:T(8,128)(2,1)}), bf16[128,8192]{0,1:T(8,128)(2,1)}) %all-gather.6.cloned.1.call-update) | async-done | bytes 2097168 | tf_op jit(solution)/shard_map/all_gather | solution.py:98
  65.4 47.4 %all-gather.8.cloned.1.call-done = bf16[128,8192]{0,1:T(8,128)(2,1)} async-done(((bf16[128,1024]{0,1:T(8,128)(2,1)}), bf16[128,8192]{0,1:T(8,128)(2,1)}) %all-gather.8.cloned.1.call-update) | async-done | bytes 2097168 | tf_op jit(solution)/shard_map/all_gather | solution.py:97
  112.9 4.1 copy.77
  116.9 54.9 %all-gather.4.cloned.1.call-done = bf16[256,128,128]{2,1,0:T(8,128)(2,1)} async-done(((bf16[64,128,128]{2,1,0:T(8,128)(2,1)}), bf16[256,128,128]{2,1,0:T(8,128)(2,1)}) %all-gather.4.cloned.1.call-update) | async-done | bytes 8388624 | tf_op jit(solution)/shard_map/all_gather | solution.py:95
  171.8 200.6 %while.12 = (s32[]{:T(128)}, bf16[16,128,128]{1,2,0:T(8,128)(2,1)S(1)}, bf16[16,128,128]{2,1,0:T(8,128)(2,1)S(1)}, pred[16,2,64]{2,1,0:T(4,128)(4,1)S(1)}, s32[1...) while((s32[]{:T(128)}, ...), condition=%wide.region_3.4_spmd, body=%wide.region_2.3_spmd.sunk | while | flops 541329536 | bytes 42345744 | solution.py:125
  171.9 6.5 %gather_fusion = bf16[128,128,128]{2,1,0:T(8,128)(2,1)} fusion(bf16[256,128,128]{2,1,0:T(8,128)(2,1)} %get-tuple-element.213, s32[1024]{0:T(1024)S(1)} %pad_clamp_fusion.4), kind=kCustom, calls=%fused_computation.clone.1 | custom fusion | bytes 8389120 | tf_op jit(solution)/shard_map/while/body/eval_jaxpr/jit(_take)/gather | solution.py:108
  184.5 6.5 %gather_fusion = bf16[128,128,128]{2,1,0:T(8,128)(2,1)} fusion(bf16[256,128,128]{2,1,0:T(8,128)(2,1)} %get-tuple-element.213, s32[1024]{0:T(1024)S(1)} %pad_clamp_fusion.4), kind=kCustom, calls=%fused_computation.clone.1 | custom fusion | bytes 8389120 | tf_op jit(solution)/shard_map/while/body/eval_jaxpr/jit(_take)/gather | solution.py:108
  197.0 6.5 %gather_fusion = bf16[128,128,128]{2,1,0:T(8,128)(2,1)} fusion(bf16[256,128,128]{2,1,0:T(8,128)(2,1)} %get-tuple-element.213, s32[1024]{0:T(1024)S(1)} %pad_clamp_fusion.4), kind=kCustom, calls=%fused_computation.clone.1 | custom fusion | bytes 8389120 | tf_op jit(solution)/shard_map/while/body/eval_jaxpr/jit(_take)/gather | solution.py:108
  209.6 6.5 %gather_fusion = bf16[128,128,128]{2,1,0:T(8,128)(2,1)} fusion(bf16[256,128,128]{2,1,0:T(8,128)(2,1)} %get-tuple-element.213, s32[1024]{0:T(1024)S(1)} %pad_clamp_fusion.4), kind=kCustom, calls=%fused_computation.clone.1 | custom fusion | bytes 8389120 | tf_op jit(solution)/shard_map/while/body/eval_jaxpr/jit(_take)/gather | solution.py:108
  222.1 6.5 %gather_fusion = bf16[128,128,128]{2,1,0:T(8,128)(2,1)} fusion(bf16[256,128,128]{2,1,0:T(8,128)(2,1)} %get-tuple-element.213, s32[1024]{0:T(1024)S(1)} %pad_clamp_fusion.4), kind=kCustom, calls=%fused_computation.clone.1 | custom fusion | bytes 8389120 | tf_op jit(solution)/shard_map/while/body/eval_jaxpr/jit(_take)/gather | solution.py:108
  234.6 6.5 %gather_fusion = bf16[128,128,128]{2,1,0:T(8,128)(2,1)} fusion(bf16[256,128,128]{2,1,0:T(8,128)(2,1)} %get-tuple-element.213, s32[1024]{0:T(1024)S(1)} %pad_clamp_fusion.4), kind=kCustom, calls=%fused_computation.clone.1 | custom fusion | bytes 8389120 | tf_op jit(solution)/shard_map/while/body/eval_jaxpr/jit(_take)/gather | solution.py:108
  247.2 6.5 %gather_fusion = bf16[128,128,128]{2,1,0:T(8,128)(2,1)} fusion(bf16[256,128,128]{2,1,0:T(8,128)(2,1)} %get-tuple-element.213, s32[1024]{0:T(1024)S(1)} %pad_clamp_fusion.4), kind=kCustom, calls=%fused_computation.clone.1 | custom fusion | bytes 8389120 | tf_op jit(solution)/shard_map/while/body/eval_jaxpr/jit(_take)/gather | solution.py:108
  259.7 6.5 %gather_fusion = bf16[128,128,128]{2,1,0:T(8,128)(2,1)} fusion(bf16[256,128,128]{2,1,0:T(8,128)(2,1)} %get-tuple-element.213, s32[1024]{0:T(1024)S(1)} %pad_clamp_fusion.4), kind=kCustom, calls=%fused_computation.clone.1 | custom fusion | bytes 8389120 | tf_op jit(solution)/shard_map/while/body/eval_jaxpr/jit(_take)/gather | solution.py:108
  272.3 6.5 %gather_fusion = bf16[128,128,128]{2,1,0:T(8,128)(2,1)} fusion(bf16[256,128,128]{2,1,0:T(8,128)(2,1)} %get-tuple-element.213, s32[1024]{0:T(1024)S(1)} %pad_clamp_fusion.4), kind=kCustom, calls=%fused_computation.clone.1 | custom fusion | bytes 8389120 | tf_op jit(solution)/shard_map/while/body/eval_jaxpr/jit(_take)/gather | solution.py:108
  284.8 6.5 %gather_fusion = bf16[128,128,128]{2,1,0:T(8,128)(2,1)} fusion(bf16[256,128,128]{2,1,0:T(8,128)(2,1)} %get-tuple-element.213, s32[1024]{0:T(1024)S(1)} %pad_clamp_fusion.4), kind=kCustom, calls=%fused_computation.clone.1 | custom fusion | bytes 8389120 | tf_op jit(solution)/shard_map/while/body/eval_jaxpr/jit(_take)/gather | solution.py:108
  297.3 6.5 %gather_fusion = bf16[128,128,128]{2,1,0:T(8,128)(2,1)} fusion(bf16[256,128,128]{2,1,0:T(8,128)(2,1)} %get-tuple-element.213, s32[1024]{0:T(1024)S(1)} %pad_clamp_fusion.4), kind=kCustom, calls=%fused_computation.clone.1 | custom fusion | bytes 8389120 | tf_op jit(solution)/shard_map/while/body/eval_jaxpr/jit(_take)/gather | solution.py:108
  309.9 6.5 %gather_fusion = bf16[128,128,128]{2,1,0:T(8,128)(2,1)} fusion(bf16[256,128,128]{2,1,0:T(8,128)(2,1)} %get-tuple-element.213, s32[1024]{0:T(1024)S(1)} %pad_clamp_fusion.4), kind=kCustom, calls=%fused_computation.clone.1 | custom fusion | bytes 8389120 | tf_op jit(solution)/shard_map/while/body/eval_jaxpr/jit(_take)/gather | solution.py:108
  322.4 6.5 %gather_fusion = bf16[128,128,128]{2,1,0:T(8,128)(2,1)} fusion(bf16[256,128,128]{2,1,0:T(8,128)(2,1)} %get-tuple-element.213, s32[1024]{0:T(1024)S(1)} %pad_clamp_fusion.4), kind=kCustom, calls=%fused_computation.clone.1 | custom fusion | bytes 8389120 | tf_op jit(solution)/shard_map/while/body/eval_jaxpr/jit(_take)/gather | solution.py:108
  334.9 6.5 %gather_fusion = bf16[128,128,128]{2,1,0:T(8,128)(2,1)} fusion(bf16[256,128,128]{2,1,0:T(8,128)(2,1)} %get-tuple-element.213, s32[1024]{0:T(1024)S(1)} %pad_clamp_fusion.4), kind=kCustom, calls=%fused_computation.clone.1 | custom fusion | bytes 8389120 | tf_op jit(solution)/shard_map/while/body/eval_jaxpr/jit(_take)/gather | solution.py:108
  347.5 6.5 %gather_fusion = bf16[128,128,128]{2,1,0:T(8,128)(2,1)} fusion(bf16[256,128,128]{2,1,0:T(8,128)(2,1)} %get-tuple-element.213, s32[1024]{0:T(1024)S(1)} %pad_clamp_fusion.4), kind=kCustom, calls=%fused_computation.clone.1 | custom fusion | bytes 8389120 | tf_op jit(solution)/shard_map/while/body/eval_jaxpr/jit(_take)/gather | solution.py:108
  360.0 6.5 %gather_fusion = bf16[128,128,128]{2,1,0:T(8,128)(2,1)} fusion(bf16[256,128,128]{2,1,0:T(8,128)(2,1)} %get-tuple-element.213, s32[1024]{0:T(1024)S(1)} %pad_clamp_fusion.4), kind=kCustom, calls=%fused_computation.clone.1 | custom fusion | bytes 8389120 | tf_op jit(solution)/shard_map/while/body/eval_jaxpr/jit(_take)/gather | solution.py:108
  372.4 24.0 %gather_fusion.1 = bf16[1024,128,128]{2,1,0:T(8,128)(2,1)} fusion(bf16[256,128,128]{2,1,0:T(8,128)(2,1)} %get-tuple-element.223, s32[1024]{0:T(1024)S(1)} %fusion.32), kind=kCustom, calls=%fused_computation.1 | custom fusion | bytes 67112960 | tf_op jit(solution)/shard_map/jit(_take)/gather | solution.py:140
  396.4 30.0 %fusion.11 = bf16[64,16,128,128]{3,1,2,0:T(8,128)(2,1)} fusion(bf16[64,16,128,128]{3,2,1,0:T(8,128)(2,1)} %bitcast.105, pred[64,16]{1,0:T(8,128)(4,1)S(1)} %compare_and_fusion.1, pred[64,16]{1,0:T(8,128)(4,1)S(1)} %copy.68), kind=kLoop, calls=%fused_computation.28 | loop fusion | flops 33554432 | bytes 67110912 | tf_op jit(solution)/shard_map/jit(_where)/select_n | solution.py:143
  426.4 20.5 %fusion.15 = bf16[8192,128]{1,0:T(8,128)(2,1)} fusion(bf16[128,2048]{0,1:T(8,128)(2,1)S(1)} %bitcast.109, bf16[1024,8,16,128]{3,2,1,0:T(8,128)(2,1)} %bitcast.106), kind=kOutput, calls=%fused_computation.31 | convolution fusion | flops 4297064448 | bytes 36175872 | tf_op jit(solution)/shard_map/dot_general | solution.py:151
  452.0 4.2 copy.81
  456.3 4.0 pad_maximum_fusion
  460.2 10.9 %gather_fusion.2 = bf16[256,128,128]{2,1,0:T(8,128)(2,1)} fusion(bf16[128,128,128]{2,0,1:T(8,128)(2,1)} %pad_maximum_fusion, s32[1024]{0:T(1024)S(1)} %pad_clamp_fusion.2), kind=kCustom, calls=%fused_computation.2 | custom fusion | bytes 16778240 | tf_op jit(solution)/shard_map/jit(_take)/gather | solution.py:138
  471.5 8.7 %gather_fusion.3 = bf16[256,128,128]{2,1,0:T(8,128)(2,1)} fusion(bf16[128,32,128]{2,0,1:T(8,128)(2,1)S(1)} %maximum_bitcast_fusion, s32[1024]{0:T(1024)S(1)} %pad_clamp_fusion.1), kind=kCustom, calls=%fused_computation.3 | custom fusion | bytes 16778240 | tf_op jit(solution)/shard_map/jit(_take)/gather | solution.py:139
  480.2 10.4 %multiply_convert_fusion.1 = bf16[256,128,128]{2,1,0:T(8,128)(2,1)} fusion(bf16[256,128,128]{2,1,0:T(8,128)(2,1)} %gather_fusion.3, bf16[256,128,128]{2,1,0:T(8,128)(2,1)} %gather_fusion.2, pred[256]{0:T(512)(128)(4,1)S(1)} %get-tuple-element.134, pred[256]{0:T(512)(128)(4,1)S(1)} %get-tuple-element.133), kind=kOutput, calls=%fused_computation.29 | convolution fusion | flops 1090519040 | bytes 25166336 | tf_op jit(solution)/shard_map/tsi,tsj->sij/dot_general | solution.py:163
  492.7 23.0 %reduce-scatter.3.cloned.1.call-done = bf16[1024,128]{1,0:T(8,128)(2,1)} async-done(((bf16[8192,128]{1,0:T(8,128)(2,1)}), bf16[1024,128]{1,0:T(8,128)(2,1)}) %reduce-scatter.3.cloned.1.call-update) | async-done | bytes 262160 | tf_op jit(solution)/shard_map/reduce_scatter | solution.py:148
  517.5 71.2 %reduce-scatter.5.cloned.1.call-done = bf16[64,128,128]{2,1,0:T(8,128)(2,1)} async-done(((bf16[256,128,128]{2,1,0:T(8,128)(2,1)}), bf16[64,128,128]{2,1,0:T(8,128)(2,1)}) %reduce-scatter.5.cloned.1.call-update) | async-done | bytes 2097168 | tf_op jit(solution)/shard_map/reduce_scatter | solution.py:160
  588.6 11.5 %fusion.28 = (f32[64,128,128]{2,1,0:T(8,128)}, f32[64,128,128]{2,1,0:T(8,128)}, f32[64,128,128]{2,1,0:T(8,128)}) fusion(f32[64,128,128]{2,1,0:T(8,128)} %param.15, bf16[64,128,128]{2,1,0:T(8,128)(2,1)} %reduce-scatter.5.cloned.1.call-done, f32[64]{0:T(128)S(1)} %convert_power_fusion, pred[64]{0:T(512)(128)(4,1)S(1)} %get-tuple-element.123, ...), kind=kLoop, calls=%fused_computation.46 | loop fusion | flops 25165824 | bytes 27264128 | tf_op jit(solution)/shard_map/jit(_where)/select_n | solution.py:71
  (309 shorter events, 116.6 us)
Async XLA Ops:
  7.2 55.3 %all-gather.6.cloned.1.call-start = ((), (), s32[]{:S(2)}) async-start(), calls=%async_computation.3 | async-start | bytes 2359296 | tf_op jit(solution)/shard_map/all_gather | solution.py:98
  9.0 103.8 %all-gather.8.cloned.1.call-start = ((), (), s32[]{:S(2)}) async-start(), calls=%async_computation.4 | async-start | bytes 2359296 | tf_op jit(solution)/shard_map/all_gather | solution.py:97
  10.9 4.1 copy-start.3
  10.9 4.8 copy-start.4
  10.9 160.9 %all-gather.4.cloned.1.call-start = ((), (), s32[]{:S(2)}) async-start(), calls=%async_computation.2 | async-start | bytes 10485760 | tf_op jit(solution)/shard_map/all_gather | solution.py:95
  14.9 500.8 %reduce-scatter.3.cloned.1.call-start = ((), (), s32[]{:S(2)}) async-start(), calls=%async_computation.5 | async-start | bytes 2359296 | tf_op jit(solution)/shard_map/reduce_scatter | solution.py:148
  181.0 1.6 copy-start
  193.6 1.6 copy-start
  206.1 1.6 copy-start
  218.6 1.6 copy-start
  231.2 1.6 copy-start
  243.7 1.6 copy-start
  256.2 1.6 copy-start
  268.8 1.6 copy-start
  281.3 1.6 copy-start
  293.9 1.6 copy-start
  306.4 1.6 copy-start
  318.9 1.6 copy-start
  331.5 1.6 copy-start
  344.0 1.6 copy-start
  356.6 1.6 copy-start
  369.1 1.6 copy-start
  426.4 20.7 %copy-start.5 = (s32[2,64,16]{1,2,0:T(8,128)S(1)}, s32[2,64,16]{1,2,0:T(8,128)}, u32[]{:S(2)}) copy-start(s32[2,64,16]{1,2,0:T(8,128)} %param.17) | copy-start | bytes 24580
  426.4 22.5 %copy-start.1 = (bf16[128,8192]{0,1:T(8,128)(2,1)S(1)}, bf16[128,8192]{0,1:T(8,128)(2,1)}, u32[]{:S(2)}) copy-start(bf16[128,8192]{0,1:T(8,128)(2,1)} %all-gather.6.cloned.1.call-done) | copy-start | bytes 6291460
  446.9 141.7 %reduce-scatter.5.cloned.1.call-start = ((), (), s32[]{:S(2)}) async-start(), calls=%async_computation.6 | async-start | bytes 10485760 | tf_op jit(solution)/shard_map/reduce_scatter | solution.py:160
  452.0 4.2 copy-start.2
Sparse Core Ops, SparseCore 0:
  10.7 51.7 all-gather.5
  65.2 47.6 all-gather.7
  115.0 56.7 all-gather.3
  447.1 68.5 reduce-scatter.2
  518.1 70.4 reduce-scatter.4
where the time goes:
time: 608 us; the launch traced here: 607 us
  waiting for transfers between devices  242 us (40%)
  local copies, waits for them, and re-layouts  198 us (33%)
  other arithmetic  94.7 us (16%)
  matrix products  55.8 us (9%)
  between operations  14.7 us (2%)
    gather x16, local copies, waits for them, and re-layouts, column_step(): jnp.take(packed, column_slots.reshape(-1), axis=0)  104 us
    reduce_scatter x1, waiting for transfers between devices, per_device(): lax.psum_scatter((scale_factor * jnp.einsum('tsi,tsj->sij', left_rows, ri...  71.2 us
    all_gather x1, waiting for transfers between devices, per_device(): lax.all_gather(packed_weight_blocks.astype(jnp.bfloat16), 'dp', axis=0, t...  54.9 us
    all_gather x1, waiting for transfers between devices, per_device(): lax.all_gather(tokens, 'tensor', axis=1, tiled=True)  47.4 us
    all_gather x1, waiting for transfers between devices, per_device(): lax.all_gather(grad_out, 'tensor', axis=1, tiled=True)  45.9 us
    select_n x16, other arithmetic, column_step(): jnp.where(column_used[:, :, None, None], blocks, jnp.zeros((), jnp.bfloat...  41.2 us
    select_n x1, other arithmetic, per_device(): jnp.where(usable[0][:, :, None, None], up_blocks, jnp.zeros((), jnp.bfloa...  30 us
    gather x1, local copies, waits for them, and re-layouts, per_device(): jnp.take(packed, slot_grid[0].reshape(-1), axis=0)  24 us
  transfers between devices with their start and end apart: 5, of which 5 were waited for; matrix products, arithmetic and copies ran while one was open for 10% of the time, Pallas kernels for 0%

commit v1 on v0

--- a/solution.py
+++ b/solution.py
@@ -1,8 +1,11 @@
+import functools
 import math
 
 import jax
 import jax.numpy as jnp
 from jax import lax
+from jax.experimental import pallas as pl
+from jax.experimental.pallas import tpu as pltpu
 from jax.sharding import PartitionSpec as P
 
 D = 8192
@@ -70,6 +73,106 @@
         jnp.where(keep_slot, new_first, first_in),
         jnp.where(keep_slot, new_second, second_in),
     )
+
+
+def gather_all(own_packed, own_left):
+    packed = lax.all_gather(own_packed, "dp", axis=0, tiled=True)
+    left_source = lax.all_gather(own_left, "tensor", axis=0, tiled=True)
+    return packed, left_source
+
+
+def reduce_all(tiles, partial_rows):
+    block_grads = lax.psum_scatter(tiles, "dp", scatter_dimension=0, tiled=True)
+    summed_rows = lax.psum_scatter(partial_rows, "tensor", scatter_dimension=0, tiled=True)
+    return block_grads.astype(jnp.float32), summed_rows.astype(jnp.float32)
+
+
+UNROLL = 4
+
+
+def forward_kernel(
+    left_at, right_at, sum_at, packed_ref, left_ref, right_ref, tiles_ref, sums, *, scale
+):
+    slot_total = packed_ref.shape[0]
+    columns = right_ref.shape[0] // 2
+
+    def clear(index, carry):
+        sums[index] = jnp.zeros(sums.shape[1:], jnp.float32)
+        return carry
+
+    lax.fori_loop(0, sums.shape[0], clear, 0)
+
+    def add_slots(step, carry):
+        base = step * UNROLL
+        parts = [
+            jnp.dot(
+                left_ref[left_at[base + k]],
+                packed_ref[base + k],
+                preferred_element_type=jnp.float32,
+            )
+            for k in range(UNROLL)
+        ]
+        for k in range(UNROLL):
+            sums[sum_at[base + k]] += parts[k]
+        return carry
+
+    lax.fori_loop(0, slot_total // UNROLL, add_slots, 0)
+
+    def activate(column, carry):
+        pre_act = scale * sums[column]
+        back_act = scale * sums[columns + column]
+        right_ref[column] = (back_act * silu_slope(pre_act)).astype(jnp.bfloat16)
+        right_ref[columns + column] = jax.nn.silu(pre_act).astype(jnp.bfloat16)
+        return carry
+
+    lax.fori_loop(0, columns, activate, 0)
+
+    def make_tiles(step, carry):
+        base = step * UNROLL
+        for k in range(UNROLL):
+            tile = lax.dot_general(
+                left_ref[left_at[base + k]],
+                right_ref[right_at[base + k]],
+                (((0,), (0,)), ((), ())),
+                preferred_element_type=jnp.float32,
+            )
+            tiles_ref[base + k] = (scale * tile).astype(jnp.bfloat16)
+        return carry
+
+    lax.fori_loop(0, slot_total // UNROLL, make_tiles, 0)
+
+
+def input_grad_kernel(right_at, row_at, up_steps, packed_ref, right_ref, out_ref, sums, *, scale):
+    rows = out_ref.shape[0]
+
+    def clear(index, carry):
+        sums[index] = jnp.zeros(sums.shape[1:], jnp.float32)
+        return carry
+
+    lax.fori_loop(0, rows, clear, 0)
+
+    def add_slots(step, carry):
+        base = step * UNROLL
+        parts = [
+            lax.dot_general(
+                right_ref[right_at[base + k]],
+                packed_ref[base + k],
+                (((1,), (1,)), ((), ())),
+                preferred_element_type=jnp.float32,
+            )
+            for k in range(UNROLL)
+        ]
+        for k in range(UNROLL):
+            sums[row_at[base + k]] += parts[k]
+        return carry
+
+    lax.fori_loop(0, up_steps[0], add_slots, 0)
+
+    def finish(index, carry):
+        out_ref[index] = (scale * sums[index]).astype(jnp.bfloat16)
+        return carry
+
+    lax.fori_loop(0, rows, finish, 0)
 
 
 def per_device(
@@ -89,83 +192,60 @@
     block_size = packed_weight_blocks.shape[1]
     row_blocks = block_mask.shape[1]
     column_blocks = block_mask.shape[2]
+    local_rows = tokens.shape[1] // block_size
     groups = lax.axis_size("dp")
     slot_total = owned_slots * groups
     step_value = step_now[0]
-    packed = lax.all_gather(packed_weight_blocks.astype(jnp.bfloat16), "dp", axis=0, tiled=True)
-    inputs_full, outgrad_full = (
-        lax.all_gather(tokens, "tensor", axis=1, tiled=True),
-        lax.all_gather(grad_out, "tensor", axis=1, tiled=True),
-    )
-    numbered, block_index, slot_regrown, slot_last, live_count = slot_table(
-        block_mask, regrown, last_step, slot_total
-    )
-    usable = (block_mask == 1) & (regrown == 0)
-    slot_grid = jnp.maximum(numbered, 0).reshape(block_mask.shape)
-
-    def column_step(accum, column_in):
-        column_slots, column_used = column_in
-        blocks = jnp.take(packed, column_slots.reshape(-1), axis=0).reshape(
-            2, row_blocks, block_size, block_size
-        )
-        blocks = jnp.where(column_used[:, :, None, None], blocks, jnp.zeros((), jnp.bfloat16))
-        dense_col = blocks.reshape(2, row_blocks * block_size, block_size)
-        pre_act = scale_factor * jnp.dot(
-            inputs_full, dense_col[0], preferred_element_type=jnp.float32
-        )
-        back_act = scale_factor * jnp.dot(
-            outgrad_full, dense_col[1], preferred_element_type=jnp.float32
-        )
-        hidden = jax.nn.silu(pre_act).astype(jnp.bfloat16)
-        hidden_grad = (back_act * silu_slope(pre_act)).astype(jnp.bfloat16)
-        return (accum, (hidden_grad, hidden))
-
-    column_inputs = (slot_grid.transpose(2, 0, 1), usable.transpose(2, 0, 1))
-    accum_shape = (1, 1)
-    accum, column_outs = lax.scan(column_step, jnp.zeros(accum_shape, jnp.float32), column_inputs)
-    grad_cols, hidden_cols = column_outs
-    left_source = jnp.concatenate(
+    own_left = jnp.concatenate(
         [
-            inputs_full.reshape(tok_count, row_blocks, block_size),
-            outgrad_full.reshape(tok_count, row_blocks, block_size),
+            tokens.reshape(tok_count, local_rows, block_size),
+            grad_out.reshape(tok_count, local_rows, block_size),
         ],
         axis=1,
-    )
-    right_source = jnp.concatenate([grad_cols, hidden_cols], axis=0).transpose(1, 0, 2)
+    ).transpose(1, 0, 2)
+    own_packed = packed_weight_blocks.astype(jnp.bfloat16)
+    packed, left_source = gather_all(own_packed, own_left)
+    _, block_index, slot_regrown, slot_last, live_count = slot_table(
+        block_mask, regrown, last_step, slot_total
+    )
     matrix_of = block_index // (row_blocks * column_blocks)
     row_of = block_index // column_blocks % row_blocks
     column_of = block_index % column_blocks
-    left_rows = jnp.take(left_source, matrix_of * row_blocks + row_of, axis=1)
-    right_rows = jnp.take(right_source, matrix_of * column_blocks + column_of, axis=1)
-    up_blocks = jnp.take(packed, slot_grid[0].reshape(-1), axis=0).reshape(
-        row_blocks, column_blocks, block_size, block_size
-    )
-    up_blocks = jnp.where(usable[0][:, :, None, None], up_blocks, jnp.zeros((), jnp.bfloat16))
-    up_dense = up_blocks.transpose(0, 2, 1, 3).reshape(
-        row_blocks * block_size, column_blocks * block_size
-    )
-    grad_flat = grad_cols.transpose(1, 0, 2).reshape(tok_count, column_blocks * block_size)
-    summed_rows = lax.psum_scatter(
-        (
-            scale_factor
-            * lax.dot_general(
-                up_dense, grad_flat, (((1,), (1,)), ((), ())), preferred_element_type=jnp.float32
-            )
-        ).astype(jnp.bfloat16),
-        "tensor",
-        scatter_dimension=0,
-        tiled=True,
-    ).astype(jnp.float32)
-    input_grad = summed_rows.T.astype(jnp.bfloat16)
-    block_grads = lax.psum_scatter(
-        (
-            scale_factor
-            * jnp.einsum("tsi,tsj->sij", left_rows, right_rows, preferred_element_type=jnp.float32)
-        ).astype(jnp.bfloat16),
-        "dp",
-        scatter_dimension=0,
-        tiled=True,
-    ).astype(jnp.float32)
+    slot_ids = jnp.arange(slot_total, dtype=jnp.int32)
+    usable = (slot_ids < live_count) & (slot_regrown == 0)
+    left_at = (row_of // local_rows * 2 + matrix_of) * local_rows + row_of % local_rows
+    right_at = matrix_of * column_blocks + column_of
+    sum_at = jnp.where(usable, right_at, 2 * column_blocks)
+    row_at = jnp.where(usable & (matrix_of == 0), row_of, row_blocks)
+    up_count = jnp.sum(block_mask[0], dtype=jnp.int32)
+    up_steps = ((up_count + UNROLL - 1) // UNROLL).reshape(1)
+    smem = pl.BlockSpec(memory_space=pltpu.SMEM)
+    vmem = pl.BlockSpec(memory_space=pltpu.VMEM)
+    params = pltpu.CompilerParams(vmem_limit_bytes=48 * 1024 * 1024)
+    block = (tok_count, block_size)
+    right_source, tiles = pl.pallas_call(
+        functools.partial(forward_kernel, scale=scale_factor),
+        out_shape=(
+            jax.ShapeDtypeStruct((2 * column_blocks,) + block, jnp.bfloat16),
+            jax.ShapeDtypeStruct((slot_total, block_size, block_size), jnp.bfloat16),
+        ),
+        in_specs=[smem] * 3 + [vmem] * 2,
+        out_specs=(vmem, vmem),
+        scratch_shapes=[pltpu.VMEM((2 * column_blocks + 1,) + block, jnp.float32)],
+        compiler_params=params,
+    )(left_at, right_at, sum_at, packed, left_source)
+    partial_rows = pl.pallas_call(
+        functools.partial(input_grad_kernel, scale=scale_factor),
+        out_shape=jax.ShapeDtypeStruct((row_blocks,) + block, jnp.bfloat16),
+        in_specs=[smem] * 3 + [vmem] * 2,
+        out_specs=vmem,
+        scratch_shapes=[pltpu.VMEM((row_blocks + 1,) + block, jnp.float32)],
+        compiler_params=params,
+    )(right_at, row_at, up_steps, packed, right_source)
+    block_grads, summed_rows = reduce_all(tiles, partial_rows)
+    input_grad = (
+        summed_rows.transpose(1, 0, 2).reshape(tok_count, tokens.shape[1]).astype(jnp.bfloat16)
+    )
     owner_first = lax.axis_index("dp") * owned_slots
     mine_regrown = lax.dynamic_slice_in_dim(slot_regrown, owner_first, owned_slots)
     mine_last = lax.dynamic_slice_in_dim(slot_last, owner_first, owned_slots)

time: 608 us -> 352 us (0.58)
  local copies, waits for them, and re-layouts: 198 us -> 8.33 us
  other arithmetic: 94.7 us -> 20.5 us
  matrix products: 55.8 us -> 0 us
  Pallas kernels: 0 us -> 46 us
  waiting for transfers between devices: 242 us -> 260 us
    gather x19 -> x0, local copies, waits for them, and re-layouts: 147 us -> none  [the longest x16 104 us: column_step(): jnp.take(packed, column_slots.reshape(-1), axis=0)]
    select_n x35 -> x2, other arithmetic: 71.4 us -> 1.31 us  [the longest x1 0.66 us: per_device(): sum_at = jnp.where(usable, right_at, 2 * column_blocks)]
    dot_general x34 -> x0, matrix products: 55.8 us -> none  [the longest x1 20.5 us: per_device(): lax.dot_general(up_dense, grad_flat, (((1,), (1,)), ((), ())), preferred_...]
    pallas_call x0 -> x2, Pallas kernels: none -> 46 us  [the longest x1 32.8 us: per_device(): pl.pallas_call(functools.partial(forward_kernel, scale=scale_factor), out...]
    reduce_scatter x2, waiting for transfers between devices: 94.2 us -> 135 us  [the longest x1 71 us: reduce_all(): block_grads = lax.psum_scatter(tiles, 'dp', scatter_dimension=0, tiled=True)]
    all_gather x3 -> x2, waiting for transfers between devices: 148 us -> 125 us  [the longest x1 65.7 us: gather_all(): left_source = lax.all_gather(own_left, 'tensor', axis=0, tiled=True)]
    while x36 -> x0, local copies, waits for them, and re-layouts: 23.3 us -> none
    slice x17 -> x1, local copies, waits for them, and re-layouts: 9.29 us -> 0.08 us  [the longest x16 9.21 us: column_step(): dense_col[0]]
  transfers between devices with their start and end apart: 5 -> 4, of which waited for: 5 -> 4; matrix products, arithmetic and copies ran while one was open for 10% -> 3% of each run, Pallas kernels for 0% -> 0%
where the time goes in v1:
time: 352 us; the launch traced here: 350 us
  waiting for transfers between devices  260 us (74%)
  Pallas kernels  46 us (13%)
  other arithmetic  20.5 us (6%)
  between operations  15.2 us (4%)
  local copies, waits for them, and re-layouts  8.33 us (2%)
    reduce_scatter x1, waiting for transfers between devices, reduce_all(): block_grads = lax.psum_scatter(tiles, 'dp', scatter_dimension=0, tiled=True)  71 us
    all_gather x1, waiting for transfers between devices, gather_all(): left_source = lax.all_gather(own_left, 'tensor', axis=0, tiled=True)  65.7 us
    reduce_scatter x1, waiting for transfers between devices, reduce_all(): lax.psum_scatter(partial_rows, 'tensor', scatter_dimension=0, tiled=True)  64 us
    all_gather x1, waiting for transfers between devices, gather_all(): packed = lax.all_gather(own_packed, 'dp', axis=0, tiled=True)  59 us
    pallas_call x1, Pallas kernels, per_device(): pl.pallas_call(functools.partial(forward_kernel, scale=scale_factor), out...  32.8 us
    pallas_call x1, Pallas kernels, per_device(): pl.pallas_call(functools.partial(input_grad_kernel, scale=scale_factor),...  13.2 us
    select_n x1, other arithmetic, adam_step(): jnp.where(keep_slot, new_second, second_in)  11.5 us
  transfers between devices with their start and end apart: 4, of which 4 were waited for; matrix products, arithmetic and copies ran while one was open for 3% of the time, Pallas kernels for 0%

profile of v1, /device:TPU:0, one launch (start us, length us, event | category | flops | bytes accessed | tf_op | source)
XLA Modules:
  0.0 350.4 jit_solution(10969486329157192508)
XLA Ops:
  7.2 1.1 copy.36
  8.3 1.1 copy.35
  9.5 1.0 copy.37
  10.6 3.9 %convert_element_type.20 = bf16[64,128,128]{2,1,0:T(8,128)(2,1)} convert(f32[64,128,128]{2,1,0:T(8,128)} %param.11) | non-fusion elementwise | flops 1048576 | bytes 6291456 | tf_op jit(solution)/shard_map/convert_element_type | solution.py:206
  14.6 0.1 copy.32
  14.7 0.6 reduce_sum.46
  15.3 0.6 slice_reduce_fusion.1
  16.6 0.1 copy.39
  16.7 0.1 broadcast_in_dim.83
  16.8 0.1 reshape.75
  16.9 0.3 reduce-window.9
  17.3 0.1 copy.33
  17.4 0.1 eq.45
  17.5 0.1 copy.34
  17.6 0.1 broadcast_in_dim.77
  17.7 0.1 slice_reduce_fusion
  17.9 1.3 select_reduce_fusion
  19.2 0.7 broadcast_select_fusion
  19.9 0.7 and_select_fusion.4.row_at
  20.5 65.7 %all-gather.5.cloned.1.call-done.left_ref = bf16[128,128,128]{2,1,0:T(8,128)(2,1)} async-done(((bf16[16,128,128]{2,1,0:T(8,128)(2,1)}), bf16[128,128,128]{2,1,0:T(8,128)(2,1)}) %all-gather.5.cloned.1.call-update) | async-done | bytes 4194320 | tf_op jit(solution)/shard_map/all_gather | solution.py:80
  86.3 59.0 %all-gather.3.cloned.1.call-done.packed_ref = bf16[256,128,128]{2,1,0:T(8,128)(2,1)} async-done(((bf16[64,128,128]{2,1,0:T(8,128)(2,1)}), bf16[256,128,128]{2,1,0:T(8,128)(2,1)}) %all-gather.3.cloned.1.call-update) | async-done | bytes 8388624 | tf_op jit(solution)/shard_map/all_gather | solution.py:79
  145.2 2.2 copy-done
  147.4 32.8 %shard_map.120 = (bf16[32,128,128]{2,1,0:T(8,128)(2,1)S(1)}, bf16[256,128,128]{2,1,0:T(8,128)(2,1)}) custom-call(s32[256]{0:T(256)S(1)} %get-tuple-element.30.left_at, s32[256]{0:T(256)S(1)} %get-tuple-element.28.right_at, s32[256]{0:T(256)S(1)} %get-tuple-element.27.sum_at, bf16[256,128,128]{2,1,0:T(8,128)(2,1)} %all-gather.3.cloned.1.call-done.packed_ref, ...), custom_call_target="tpu_custom_call" | custom-call | tf_op jit(solution)/shard_map/pallas_call | solution.py:226
  180.3 13.2 %shard_map.121 = bf16[64,128,128]{2,1,0:T(8,128)(2,1)} custom-call(s32[256]{0:T(256)S(1)} %get-tuple-element.28.right_at, s32[256]{0:T(256)S(1)} %and_select_fusion.4.row_at, s32[1]{0:T(128)} %bitcast.1.up_steps, bf16[256,128,128]{2,1,0:T(8,128)(2,1)} %all-gather.3.cloned.1.call-done.packed_ref, bf16[32,128,128]{2,1,0:T(8,128)(2,1)S(1)} %get-tuple-element.6.right_ref), custom_call_target="tpu_custom_call" | custom-call | tf_op jit(solution)/shard_map/pallas_call | solution.py:237
  193.5 0.5 reduce-scatter.5.cloned.1.call-update
  194.7 0.7 add_compare_fusion
  195.3 0.1 power_subtract_fusion.1
  195.5 64.0 %reduce-scatter.3.cloned.1.call-done = bf16[8,128,128]{2,1,0:T(8,128)(2,1)} async-done(((bf16[64,128,128]{2,1,0:T(8,128)(2,1)}), bf16[8,128,128]{2,1,0:T(8,128)(2,1)}) %reduce-scatter.3.cloned.1.call-update) | async-done | bytes 262160 | tf_op jit(solution)/shard_map/reduce_scatter | solution.py:86
  259.5 1.1 copy.38
  260.6 0.9 copy.40
  261.4 71.0 %reduce-scatter.5.cloned.1.call-done = bf16[64,128,128]{2,1,0:T(8,128)(2,1)} async-done(((bf16[256,128,128]{2,1,0:T(8,128)(2,1)}), bf16[64,128,128]{2,1,0:T(8,128)(2,1)}) %reduce-scatter.5.cloned.1.call-update) | async-done | bytes 2097168 | tf_op jit(solution)/shard_map/reduce_scatter | solution.py:85
  332.5 11.5 %fusion.3 = (f32[64,128,128]{2,1,0:T(8,128)}, f32[64,128,128]{2,1,0:T(8,128)}, f32[64,128,128]{2,1,0:T(8,128)}) fusion(f32[64,128,128]{2,1,0:T(8,128)} %param.13, bf16[64,128,128]{2,1,0:T(8,128)(2,1)} %reduce-scatter.5.cloned.1.call-done, f32[64]{0:T(128)S(1)} %convert_power_fusion, pred[64]{0:T(512)(128)(4,1)S(1)} %get-tuple-element.26, ...), kind=kLoop, calls=%fused_computation.6 | loop fusion | flops 25165824 | bytes 27264128 | tf_op jit(solution)/shard_map/jit(_where)/select_n | solution.py:74
  (22 shorter events, 0.5 us)
Async XLA Ops:
  7.2 79.1 %all-gather.5.cloned.1.call-start = ((), (), s32[]{:S(2)}) async-start(), calls=%async_computation.3 | async-start | bytes 4718592 | tf_op jit(solution)/shard_map/all_gather | solution.py:80
  10.6 4.1 %copy-start.1 = (s32[2,64,16]{1,2,0:T(8,128)S(1)}, s32[2,64,16]{1,2,0:T(8,128)}, u32[]{:S(2)}) copy-start(s32[2,64,16]{1,2,0:T(8,128)} %param.14) | copy-start | bytes 24580
  10.6 6.1 %copy-start.2 = (s32[2,64,16]{1,2,0:T(8,128)S(1)}, s32[2,64,16]{1,2,0:T(8,128)}, u32[]{:S(2)}) copy-start(s32[2,64,16]{1,2,0:T(8,128)} %param.15) | copy-start | bytes 24580
  10.6 6.9 %copy-start.3 = (s32[2,64,16]{1,2,0:T(8,128)S(1)}, s32[2,64,16]{1,2,0:T(8,128)}, u32[]{:S(2)}) copy-start(s32[2,64,16]{1,2,0:T(8,128)} %param.16) | copy-start | bytes 24580
  10.6 134.6 %all-gather.3.cloned.1.call-start = ((), (), s32[]{:S(2)}) async-start(), calls=%async_computation.2 | async-start | bytes 10485760 | tf_op jit(solution)/shard_map/all_gather | solution.py:79
  14.6 244.9 %reduce-scatter.3.cloned.1.call-start = ((), (), s32[]{:S(2)}) async-start(), calls=%async_computation.4 | async-start | bytes 2359296 | tf_op jit(solution)/shard_map/reduce_scatter | solution.py:86
  145.2 2.2 copy-start
  193.5 139.0 %reduce-scatter.5.cloned.1.call-start = ((), (), s32[]{:S(2)}) async-start(), calls=%async_computation.5 | async-start | bytes 10485760 | tf_op jit(solution)/shard_map/reduce_scatter | solution.py:85
Sparse Core Ops, SparseCore 0:
  10.7 75.5 all-gather.4
  88.4 56.7 all-gather.2
  193.6 65.8 reduce-scatter.2
  261.9 70.5 reduce-scatter.4

commit v2 on v1

--- a/solution.py
+++ b/solution.py
@@ -75,16 +75,332 @@
     )
 
 
+INNER = 2
+
+
+def piece(index, chunk, chunks, shard):
+    size = shard // chunks
+    return pl.ds((index * chunks + chunk) * size, size)
+
+
+def remote(src, dst, send_sem, recv_sem, axis, target):
+    return pltpu.make_async_remote_copy(
+        src_ref=src,
+        dst_ref=dst,
+        send_sem=send_sem,
+        recv_sem=recv_sem,
+        device_id={axis: target},
+        device_id_type=pl.DeviceIdType.MESH,
+    )
+
+
+def greet(targets):
+    barrier = pltpu.get_barrier_semaphore()
+    for axis, target, exists in targets:
+
+        @pl.when(exists)
+        def _(axis=axis, target=target):
+            pl.semaphore_signal(
+                barrier, inc=1, device_id={axis: target}, device_id_type=pl.DeviceIdType.MESH
+            )
+
+    pl.semaphore_wait(barrier, sum(jnp.where(exists, 1, 0) for _, _, exists in targets))
+
+
+class LineGather:
+    def __init__(self, axis, size, chunks, own, out, sems):
+        self.axis, self.chunks, self.own, self.out = axis, chunks, own, out
+        self.recv, self.up, self.down, self.across, self.local = sems
+        self.outer = size // INNER
+        me = lax.axis_index(axis)
+        self.me, self.mine, self.inner = me, me // INNER, me % INNER
+        self.shard = own.shape[0]
+
+    def targets(self):
+        mine = self.mine
+        return [
+            (self.axis, self.me + INNER, mine + 1 < self.outer),
+            (self.axis, self.me - INNER, mine > 0),
+            (self.axis, mine * INNER + 1 - self.inner, mine >= 0),
+        ]
+
+    def copy(self, source, chunk, way, inner=None):
+        inner = self.inner if inner is None else inner
+        index = source * INNER + inner
+        at = self.out.at[piece(index, chunk, self.chunks, self.shard)]
+        slot = source * self.chunks + chunk
+        sem, target = {
+            "up": (self.up, self.me + INNER),
+            "down": (self.down, self.me - INNER),
+            "across": (self.across, self.mine * INNER + 1 - self.inner),
+        }[way]
+        recv = self.recv.at[index * self.chunks + chunk]
+        return at, sem.at[slot], recv, target
+
+    def send(self, source, chunk, way, own=False):
+        at, sem, recv, target = self.copy(source, chunk, way)
+        src = self.own.at[piece(0, chunk, self.chunks, self.shard)] if own else at
+        remote(src, at, sem, recv, self.axis, target).start()
+
+    def wait_send(self, source, chunk, way):
+        at, sem, recv, target = self.copy(source, chunk, way)
+        remote(at, at, sem, recv, self.axis, target).wait_send()
+
+    def wait_recv(self, source, chunk, inner):
+        at, sem, recv, target = self.copy(source, chunk, "across", inner)
+        remote(at, at, sem, recv, self.axis, target).wait_recv()
+
+    def own_copy(self):
+        at = self.out.at[pl.ds(self.me * self.shard, self.shard)]
+        return pltpu.make_async_copy(self.own, at, self.local)
+
+    def begin(self, chunk):
+        mine = self.mine
+
+        @pl.when(mine + 1 < self.outer)
+        def _():
+            self.send(mine, chunk, "up", own=True)
+
+        @pl.when(mine > 0)
+        def _():
+            self.send(mine, chunk, "down", own=True)
+
+        self.send(mine, chunk, "across", own=True)
+
+    def step(self, distance, chunk):
+        low, high = self.mine - distance, self.mine + distance
+
+        @pl.when(low >= 0)
+        def _():
+            self.wait_recv(low, chunk, self.inner)
+
+            @pl.when(self.mine + 1 < self.outer)
+            def _():
+                self.send(low, chunk, "up")
+
+            self.send(low, chunk, "across")
+
+        @pl.when(high < self.outer)
+        def _():
+            self.wait_recv(high, chunk, self.inner)
+
+            @pl.when(self.mine > 0)
+            def _():
+                self.send(high, chunk, "down")
+
+            self.send(high, chunk, "across")
+
+    def finish(self):
+        for source in range(self.outer):
+            for chunk in range(self.chunks):
+                self.wait_recv(source, chunk, 1 - self.inner)
+                self.wait_send(source, chunk, "across")
+
+                @pl.when((self.mine >= source) & (self.mine + 1 < self.outer))
+                def _(source=source, chunk=chunk):
+                    self.wait_send(source, chunk, "up")
+
+                @pl.when((self.mine <= source) & (self.mine > 0))
+                def _(source=source, chunk=chunk):
+                    self.wait_send(source, chunk, "down")
+
+        self.own_copy().wait()
+
+
+def gather_kernel(sizes, chunk_counts, own_packed, own_left, packed_out, left_out, *sems):
+    lines = [
+        LineGather("dp", sizes[0], chunk_counts[0], own_packed, packed_out, sems[:5]),
+        LineGather("tensor", sizes[1], chunk_counts[1], own_left, left_out, sems[5:]),
+    ]
+    greet(lines[0].targets() + lines[1].targets())
+    events = []
+    for line in lines:
+        for chunk in range(line.chunks):
+            events.append((chunk / line.chunks, line, 0, chunk))
+            for distance in range(1, line.outer):
+                when = 1 + (distance - 1 + (chunk + 1) / line.chunks) / (line.outer - 1)
+                events.append((when, line, distance, chunk))
+    events.sort(key=lambda event: event[0])
+    for when, line, distance, chunk in events:
+        if distance == 0:
+            line.begin(chunk)
+    for line in lines:
+        line.own_copy().start()
+    for when, line, distance, chunk in events:
+        if distance > 0:
+            line.step(distance, chunk)
+    for line in lines:
+        line.finish()
+
+
+def line_sems(size, chunks):
+    dma = pltpu.SemaphoreType.DMA
+    outer = size // INNER
+    return [dma((size * chunks,))] + [dma((outer * chunks,))] * 3 + [dma]
+
+
 def gather_all(own_packed, own_left):
-    packed = lax.all_gather(own_packed, "dp", axis=0, tiled=True)
-    left_source = lax.all_gather(own_left, "tensor", axis=0, tiled=True)
-    return packed, left_source
+    sizes = (lax.axis_size("dp"), lax.axis_size("tensor"))
+    chunk_counts = (math.gcd(4, own_packed.shape[0]), math.gcd(2, own_left.shape[0]))
+    vmem = pl.BlockSpec(memory_space=pltpu.VMEM)
+    return pl.pallas_call(
+        functools.partial(gather_kernel, sizes, chunk_counts),
+        out_shape=(
+            jax.ShapeDtypeStruct((sizes[0] * own_packed.shape[0],) + own_packed.shape[1:], jnp.bfloat16),
+            jax.ShapeDtypeStruct((sizes[1] * own_left.shape[0],) + own_left.shape[1:], jnp.bfloat16),
+        ),
+        in_specs=[vmem, vmem],
+        out_specs=(pl.BlockSpec(memory_space=pl.ANY), pl.BlockSpec(memory_space=pl.ANY)),
+        scratch_shapes=line_sems(sizes[0], chunk_counts[0]) + line_sems(sizes[1], chunk_counts[1]),
+        compiler_params=pltpu.CompilerParams(
+            collective_id=0, has_side_effects=True, vmem_limit_bytes=48 * 1024 * 1024
+        ),
+    )(own_packed, own_left)
+
+
+class PairReduce:
+    def __init__(self, axis, size, chunks, data, out, near, far, sems):
+        self.axis, self.chunks, self.data, self.out = axis, chunks, data, out
+        self.near, self.far = near, far
+        self.near_send, self.near_recv, self.far_send, self.far_recv = sems
+        self.outer = size // INNER
+        me = lax.axis_index(axis)
+        self.me, self.mine, self.inner = me, me // INNER, me % INNER
+        self.shard = out.shape[0]
+
+    def owner(self, offset):
+        return lax.rem(self.mine + offset, self.outer)
+
+    def targets(self):
+        far = [
+            (self.axis, self.owner(offset) * INNER + self.inner, self.mine >= 0)
+            for offset in range(1, self.outer)
+        ]
+        return far + [(self.axis, self.mine * INNER + 1 - self.inner, self.mine >= 0)]
+
+    def near_copy(self, offset, chunk):
+        owner = self.owner(offset)
+        other = 1 - self.inner
+        slot = owner * self.chunks + chunk
+        return remote(
+            self.data.at[piece(owner * INNER + other, chunk, self.chunks, self.shard)],
+            self.near.at[piece(owner, chunk, self.chunks, self.shard)],
+            self.near_send.at[slot],
+            self.near_recv.at[slot],
+            self.axis,
+            self.mine * INNER + other,
+        )
+
+    def far_copy(self, offset, chunk):
+        owner = self.owner(offset)
+        return remote(
+            self.near.at[piece(owner, chunk, self.chunks, self.shard)],
+            self.far.at[piece(offset - 1, chunk, self.chunks, self.shard)],
+            self.far_send.at[(offset - 1) * self.chunks + chunk],
+            self.far_recv.at[(offset - 1) * self.chunks + chunk],
+            self.axis,
+            owner * INNER + self.inner,
+        )
+
+    def send_pair(self, offset, chunk):
+        self.near_copy(offset, chunk).wait_recv()
+        owner = self.owner(offset)
+        size = self.shard // self.chunks
+        near_at = (owner * self.chunks + chunk) * size
+        data_at = ((owner * INNER + self.inner) * self.chunks + chunk) * size
+
+        def add(index, carry):
+            total = self.near[near_at + index].astype(jnp.float32)
+            total += self.data[data_at + index].astype(jnp.float32)
+            self.near[near_at + index] = total.astype(jnp.bfloat16)
+            return carry
+
+        lax.fori_loop(0, size, add, 0)
+        self.far_copy(offset, chunk).start()
+
+    def total(self, chunk):
+        self.near_copy(0, chunk).wait_recv()
+        for offset in range(1, self.outer):
+            self.far_copy(offset, chunk).wait_recv()
+        size = self.shard // self.chunks
+        near_at = (self.mine * self.chunks + chunk) * size
+        data_at = (self.me * self.chunks + chunk) * size
+
+        def add(index, carry):
+            total = self.near[near_at + index].astype(jnp.float32)
+            total += self.data[data_at + index].astype(jnp.float32)
+            for offset in range(1, self.outer):
+                at = ((offset - 1) * self.chunks + chunk) * size
+                total += self.far[at + index].astype(jnp.float32)
+            self.out[chunk * size + index] = total.astype(self.out.dtype)
+            return carry
+
+        lax.fori_loop(0, size, add, 0)
+
+    def finish(self):
+        for chunk in range(self.chunks):
+            for offset in range(self.outer):
+                self.near_copy(offset, chunk).wait_send()
+                if offset > 0:
+                    self.far_copy(offset, chunk).wait_send()
+
+
+def reduce_kernel(sizes, chunk_counts, tiles, rows, grads_out, rows_out, *scratch):
+    wide = PairReduce(
+        "dp", sizes[0], chunk_counts[0], tiles, grads_out, scratch[0], scratch[1], scratch[4:8]
+    )
+    thin = PairReduce(
+        "tensor", sizes[1], chunk_counts[1], rows, rows_out, scratch[2], scratch[3], scratch[8:]
+    )
+    greet(wide.targets() + thin.targets())
+    for line in (wide, thin):
+        for offset in list(range(1, line.outer)) + [0]:
+            for chunk in range(line.chunks):
+                line.near_copy(offset, chunk).start()
+    for line in (wide, thin):
+        for offset in range(1, line.outer):
+            for chunk in range(line.chunks):
+                line.send_pair(offset, chunk)
+    for chunk in range(wide.chunks - 1):
+        wide.total(chunk)
+    for chunk in range(thin.chunks):
+        thin.total(chunk)
+    wide.total(wide.chunks - 1)
+    wide.finish()
+    thin.finish()
+
+
+def pair_sems(size, chunks):
+    dma = pltpu.SemaphoreType.DMA
+    outer = size // INNER
+    return [dma((outer * chunks,))] * 2 + [dma((max(outer - 1, 1) * chunks,))] * 2
 
 
 def reduce_all(tiles, partial_rows):
-    block_grads = lax.psum_scatter(tiles, "dp", scatter_dimension=0, tiled=True)
-    summed_rows = lax.psum_scatter(partial_rows, "tensor", scatter_dimension=0, tiled=True)
-    return block_grads.astype(jnp.float32), summed_rows.astype(jnp.float32)
+    sizes = (lax.axis_size("dp"), lax.axis_size("tensor"))
+    shards = (tiles.shape[0] // sizes[0], partial_rows.shape[0] // sizes[1])
+    chunk_counts = (math.gcd(4, shards[0]), math.gcd(2, shards[1]))
+    vmem = pl.BlockSpec(memory_space=pltpu.VMEM)
+    scratch = []
+    for array, size, shard in zip((tiles, partial_rows), sizes, shards):
+        outer = size // INNER
+        scratch.append(pltpu.VMEM((outer * shard,) + array.shape[1:], jnp.bfloat16))
+        scratch.append(pltpu.VMEM((max(outer - 1, 1) * shard,) + array.shape[1:], jnp.bfloat16))
+    return pl.pallas_call(
+        functools.partial(reduce_kernel, sizes, chunk_counts),
+        out_shape=(
+            jax.ShapeDtypeStruct((shards[0],) + tiles.shape[1:], jnp.float32),
+            jax.ShapeDtypeStruct((shards[1],) + partial_rows.shape[1:], jnp.bfloat16),
+        ),
+        in_specs=[vmem, vmem],
+        out_specs=(vmem, vmem),
+        scratch_shapes=scratch
+        + pair_sems(sizes[0], chunk_counts[0])
+        + pair_sems(sizes[1], chunk_counts[1]),
+        compiler_params=pltpu.CompilerParams(
+            collective_id=1, has_side_effects=True, vmem_limit_bytes=48 * 1024 * 1024
+        ),
+    )(tiles, partial_rows)
 
 
 UNROLL = 4

time: 352 us -> 188 us (0.53)
  waiting for transfers between devices: 260 us -> 0 us
  Pallas kernels: 46 us -> 157 us
  between operations: 15.2 us -> 2.11 us
    reduce_scatter x2 -> x0, waiting for transfers between devices: 135 us -> none  [the longest x1 71 us: reduce_all(): block_grads = lax.psum_scatter(tiles, 'dp', scatter_dimension=0, tiled=True)]
    all_gather x2 -> x0, waiting for transfers between devices: 125 us -> none  [the longest x1 65.7 us: gather_all(): left_source = lax.all_gather(own_left, 'tensor', axis=0, tiled=True)]
    pallas_call x0 -> x2, Pallas kernels: none -> 112 us  [the longest x1 58.1 us: gather_all(): pl.pallas_call(functools.partial(gather_kernel, sizes, chunk_counts), out...]
  transfers between devices with their start and end apart: 4 -> 0, of which waited for: 4 -> 0; matrix products, arithmetic and copies ran while one was open for 3% -> 0% of each run, Pallas kernels for 0% -> 0%
where the time goes in v2:
time: 188 us; the launch traced here: 187 us
  Pallas kernels  157 us (84%)
  other arithmetic  20.7 us (11%)
  local copies, waits for them, and re-layouts  7.04 us (4%)
  between operations  2.11 us (1%)
    pallas_call x1, Pallas kernels, gather_all(): pl.pallas_call(functools.partial(gather_kernel, sizes, chunk_counts), out...  58.1 us
    pallas_call x1, Pallas kernels, reduce_all(): pl.pallas_call(functools.partial(reduce_kernel, sizes, chunk_counts), out...  54.3 us
    pallas_call x1, Pallas kernels, per_device(): pl.pallas_call(functools.partial(forward_kernel, scale=scale_factor), out...  33.1 us
    select_n x1, other arithmetic, adam_step(): jnp.where(keep_slot, new_second, second_in)  11.6 us
    pallas_call x1, Pallas kernels, per_device(): pl.pallas_call(functools.partial(input_grad_kernel, scale=scale_factor),...  11.4 us
    unnamed x14, local copies, waits for them, and re-layouts  5.85 us

profile of v2, /device:TPU:0, one launch (start us, length us, event | category | flops | bytes accessed | tf_op | source)
XLA Modules:
  0.0 186.8 jit_solution(11153521258330474919)
XLA Ops:
  0.7 0.9 copy.23
  1.5 0.1 reshape.76
  1.6 0.3 reduce-window.9
  1.9 0.1 slice.13
  2.0 0.1 slice_reduce_fusion
  2.2 0.8 copy.25
  3.0 0.1 broadcast_in_dim.77
  3.1 0.8 copy.31
  3.9 0.1 broadcast_in_dim.83
  4.0 0.7 broadcast_compare_fusion
  4.7 0.1 copy.24
  4.8 0.1 eq.45
  4.9 1.3 select_reduce_fusion
  6.2 1.4 reduce_sum.46
  7.6 0.7 and_select_fusion
  8.2 0.7 broadcast_select_fusion
  8.9 2.6 %convert_element_type.9.own_packed = bf16[64,128,128]{2,1,0:T(8,128)(2,1)S(1)} convert(f32[64,128,128]{2,1,0:T(8,128)} %param.11) | non-fusion elementwise | flops 1048576 | bytes 6291456 | tf_op jit(solution)/shard_map/convert_element_type | solution.py:522
  11.5 0.2 copy.26
  11.6 0.2 copy.28
  11.8 0.2 copy.27
  12.0 0.2 copy.29
  12.3 58.1 %shard_map.120 = (bf16[256,128,128]{2,1,0:T(8,128)(2,1)}, bf16[128,128,128]{2,1,0:T(8,128)(2,1)}) custom-call(bf16[64,128,128]{2,1,0:T(8,128)(2,1)S(1)} %convert_element_type.9.own_packed, bf16[16,128,128]{2,1,0:T(8,128)(2,1)S(1)} %maximum_bitcast_fusion.own_left), custom_call_target="tpu_custom_call" | custom-call | tf_op jit(solution)/shard_map/pallas_call | solution.py:246
  70.4 2.2 %copy-done = bf16[128,128,128]{2,1,0:T(8,128)(2,1)S(1)} copy-done((bf16[128,128,128]{2,1,0:T(8,128)(2,1)S(1)}, bf16[128,128,128]{2,1,0:T(8,128)(2,1)}, u32[]{:S(2)}) %copy-start) | copy-done | bytes 4194328
  72.6 33.1 %shard_map.121 = (bf16[32,128,128]{2,1,0:T(8,128)(2,1)S(1)}, bf16[256,128,128]{2,1,0:T(8,128)(2,1)}) custom-call(s32[256]{0:T(256)S(1)} %get-tuple-element.39.left_at, s32[256]{0:T(256)S(1)} %get-tuple-element.35.right_at, s32[256]{0:T(256)S(1)} %get-tuple-element.34.sum_at, bf16[256,128,128]{2,1,0:T(8,128)(2,1)} %get-tuple-element.10.packed_ref, ...), custom_call_target="tpu_custom_call" | custom-call | tf_op jit(solution)/shard_map/pallas_call | solution.py:542
  105.7 0.6 slice_reduce_fusion.1
  107.0 11.4 %shard_map.122.rows = bf16[64,128,128]{2,1,0:T(8,128)(2,1)S(1)} custom-call(s32[256]{0:T(256)S(1)} %get-tuple-element.35.right_at, s32[256]{0:T(256)S(1)} %get-tuple-element.31.row_at, s32[1]{0:T(128)} %bitcast.4.up_steps, bf16[256,128,128]{2,1,0:T(8,128)(2,1)} %get-tuple-element.10.packed_ref, bf16[32,128,128]{2,1,0:T(8,128)(2,1)S(1)} %get-tuple-element.13.right_ref), custom_call_target="tpu_custom_call" | custom-call | tf_op jit(solution)/shard_map/pallas_call | solution.py:553
  118.4 54.3 %shard_map.123 = (f32[64,128,128]{2,1,0:T(8,128)}, bf16[8,128,128]{2,1,0:T(8,128)(2,1)S(1)}) custom-call(bf16[256,128,128]{2,1,0:T(8,128)(2,1)} %get-tuple-element.12.tiles, bf16[64,128,128]{2,1,0:T(8,128)(2,1)S(1)} %shard_map.122.rows), custom_call_target="tpu_custom_call" | custom-call | tf_op jit(solution)/shard_map/pallas_call | solution.py:389
  173.4 0.1 power_subtract_fusion.1
  173.5 0.7 add_compare_fusion
  174.1 11.6 %fusion.2 = (f32[64,128,128]{2,1,0:T(8,128)}, f32[64,128,128]{2,1,0:T(8,128)}, f32[64,128,128]{2,1,0:T(8,128)}) fusion(f32[64,128,128]{2,1,0:T(8,128)} %param.13, f32[64,128,128]{2,1,0:T(8,128)} %get-tuple-element.15, f32[64]{0:T(128)S(1)} %convert_power_fusion, pred[64]{0:T(512)(128)(4,1)S(1)} %get-tuple-element.30, pred[64]{0:T(512)(128)(4,1)S(1)} %add_compare_fusion, ...), kind=kLoop, calls=%fused_computation.5 | loop fusion | flops 24117248 | bytes 29361280 | tf_op jit(solution)/shard_map/jit(_where)/select_n | solution.py:74
  185.8 0.2 copy.30
  186.0 0.9 copy.32
  (12 shorter events, 0.2 us)
Async XLA Ops:
  0.6 10.8 %copy-start.1 = (bf16[128,1024]{1,0:T(8,128)(2,1)S(1)}, bf16[128,1024]{1,0:T(8,128)(2,1)}, u32[]{:S(2)}) copy-start(bf16[128,1024]{1,0:T(8,128)(2,1)} %param.9) | copy-start | bytes 786436
  0.6 11.2 %copy-start.2 = (bf16[128,1024]{1,0:T(8,128)(2,1)S(1)}, bf16[128,1024]{1,0:T(8,128)(2,1)}, u32[]{:S(2)}) copy-start(bf16[128,1024]{1,0:T(8,128)(2,1)} %param.10) | copy-start | bytes 786436
  70.4 2.2 %copy-start = (bf16[128,128,128]{2,1,0:T(8,128)(2,1)S(1)}, bf16[128,128,128]{2,1,0:T(8,128)(2,1)}, u32[]{:S(2)}) copy-start(bf16[128,128,128]{2,1,0:T(8,128)(2,1)} %get-tuple-element.11.left_ref) | copy-start | bytes 12582916
  72.6 33.1 %copy-start.3 = (s32[2,64,16]{1,2,0:T(8,128)S(1)}, s32[2,64,16]{1,2,0:T(8,128)}, u32[]{:S(2)}) copy-start(s32[2,64,16]{1,2,0:T(8,128)} %param.14) | copy-start | bytes 24580

commit v3 on v2

--- a/solution.py
+++ b/solution.py
@@ -345,7 +345,38 @@
                     self.far_copy(offset, chunk).wait_send()
 
 
-def reduce_kernel(sizes, chunk_counts, tiles, rows, grads_out, rows_out, *scratch):
+def make_tiles(left_at, right_at, left_ref, right_ref, tiles_ref, first, count, scale):
+    unroll = math.gcd(UNROLL, count)
+
+    def step(index, carry):
+        base = first + index * unroll
+        for k in range(unroll):
+            tile = lax.dot_general(
+                left_ref[left_at[base + k]],
+                right_ref[right_at[base + k]],
+                (((0,), (0,)), ((), ())),
+                preferred_element_type=jnp.float32,
+            )
+            tiles_ref[base + k] = (scale * tile).astype(jnp.bfloat16)
+        return carry
+
+    lax.fori_loop(0, count // unroll, step, 0)
+
+
+def reduce_kernel(
+    sizes,
+    chunk_counts,
+    scale,
+    left_at,
+    right_at,
+    left_ref,
+    right_ref,
+    rows,
+    grads_out,
+    rows_out,
+    tiles,
+    *scratch,
+):
     wide = PairReduce(
         "dp", sizes[0], chunk_counts[0], tiles, grads_out, scratch[0], scratch[1], scratch[4:8]
     )
@@ -353,14 +384,25 @@
         "tensor", sizes[1], chunk_counts[1], rows, rows_out, scratch[2], scratch[3], scratch[8:]
     )
     greet(wide.targets() + thin.targets())
-    for line in (wide, thin):
-        for offset in list(range(1, line.outer)) + [0]:
-            for chunk in range(line.chunks):
-                line.near_copy(offset, chunk).start()
-    for line in (wide, thin):
-        for offset in range(1, line.outer):
-            for chunk in range(line.chunks):
-                line.send_pair(offset, chunk)
+    for offset in list(range(1, thin.outer)) + [0]:
+        for chunk in range(thin.chunks):
+            thin.near_copy(offset, chunk).start()
+    size = wide.shard // wide.chunks
+    thin_pairs = [(o, k) for o in range(1, thin.outer) for k in range(thin.chunks)]
+    wide_steps = [(o, k) for o in list(range(1, wide.outer)) + [0] for k in range(wide.chunks)]
+    for at, (offset, chunk) in enumerate(wide_steps):
+        owner = wide.owner(offset)
+        for inner in (1 - wide.inner, wide.inner):
+            first = ((owner * INNER + inner) * wide.chunks + chunk) * size
+            make_tiles(left_at, right_at, left_ref, right_ref, tiles, first, size, scale)
+            if inner is not wide.inner:
+                wide.near_copy(offset, chunk).start()
+        if offset > 0:
+            wide.send_pair(offset, chunk)
+        low = at * len(thin_pairs) // len(wide_steps)
+        high = (at + 1) * len(thin_pairs) // len(wide_steps)
+        for pair in thin_pairs[low:high]:
+            thin.send_pair(*pair)
     for chunk in range(wide.chunks - 1):
         wide.total(chunk)
     for chunk in range(thin.chunks):
@@ -376,23 +418,26 @@
     return [dma((outer * chunks,))] * 2 + [dma((max(outer - 1, 1) * chunks,))] * 2
 
 
-def reduce_all(tiles, partial_rows):
+def reduce_all(left_at, right_at, left_source, right_source, partial_rows, scale):
     sizes = (lax.axis_size("dp"), lax.axis_size("tensor"))
-    shards = (tiles.shape[0] // sizes[0], partial_rows.shape[0] // sizes[1])
+    side = left_source.shape[2]
+    tile_shape = (left_at.shape[0], side, side)
+    shards = (tile_shape[0] // sizes[0], partial_rows.shape[0] // sizes[1])
     chunk_counts = (math.gcd(4, shards[0]), math.gcd(2, shards[1]))
     vmem = pl.BlockSpec(memory_space=pltpu.VMEM)
-    scratch = []
-    for array, size, shard in zip((tiles, partial_rows), sizes, shards):
+    smem = pl.BlockSpec(memory_space=pltpu.SMEM)
+    scratch = [pltpu.VMEM(tile_shape, jnp.bfloat16)]
+    for shape, size, shard in zip((tile_shape, partial_rows.shape), sizes, shards):
         outer = size // INNER
-        scratch.append(pltpu.VMEM((outer * shard,) + array.shape[1:], jnp.bfloat16))
-        scratch.append(pltpu.VMEM((max(outer - 1, 1) * shard,) + array.shape[1:], jnp.bfloat16))
+        scratch.append(pltpu.VMEM((outer * shard,) + shape[1:], jnp.bfloat16))
+        scratch.append(pltpu.VMEM((max(outer - 1, 1) * shard,) + shape[1:], jnp.bfloat16))
     return pl.pallas_call(
-        functools.partial(reduce_kernel, sizes, chunk_counts),
+        functools.partial(reduce_kernel, sizes, chunk_counts, scale),
         out_shape=(
-            jax.ShapeDtypeStruct((shards[0],) + tiles.shape[1:], jnp.float32),
+            jax.ShapeDtypeStruct((shards[0],) + tile_shape[1:], jnp.float32),
             jax.ShapeDtypeStruct((shards[1],) + partial_rows.shape[1:], jnp.bfloat16),
         ),
-        in_specs=[vmem, vmem],
+        in_specs=[smem, smem, vmem, vmem, vmem],
         out_specs=(vmem, vmem),
         scratch_shapes=scratch
         + pair_sems(sizes[0], chunk_counts[0])
@@ -400,14 +445,26 @@
         compiler_params=pltpu.CompilerParams(
             collective_id=1, has_side_effects=True, vmem_limit_bytes=48 * 1024 * 1024
         ),
-    )(tiles, partial_rows)
+    )(left_at, right_at, left_source, right_source, partial_rows)
 
 
 UNROLL = 4
 
 
 def forward_kernel(
-    left_at, right_at, sum_at, packed_ref, left_ref, right_ref, tiles_ref, sums, *, scale
+    left_at,
+    right_at,
+    sum_at,
+    row_at,
+    up_steps,
+    packed_ref,
+    left_ref,
+    right_ref,
+    out_ref,
+    sums,
+    row_sums,
+    *,
+    scale,
 ):
     slot_total = packed_ref.shape[0]
     columns = right_ref.shape[0] // 2
@@ -443,22 +500,10 @@
 
     lax.fori_loop(0, columns, activate, 0)
 
-    def make_tiles(step, carry):
-        base = step * UNROLL
-        for k in range(UNROLL):
-            tile = lax.dot_general(
-                left_ref[left_at[base + k]],
-                right_ref[right_at[base + k]],
-                (((0,), (0,)), ((), ())),
-                preferred_element_type=jnp.float32,
-            )
-            tiles_ref[base + k] = (scale * tile).astype(jnp.bfloat16)
-        return carry
-
-    lax.fori_loop(0, slot_total // UNROLL, make_tiles, 0)
-
-
-def input_grad_kernel(right_at, row_at, up_steps, packed_ref, right_ref, out_ref, sums, *, scale):
+    add_input_grad(right_at, row_at, up_steps, packed_ref, right_ref, out_ref, row_sums, scale)
+
+
+def add_input_grad(right_at, row_at, up_steps, packed_ref, right_ref, out_ref, sums, scale):
     rows = out_ref.shape[0]
 
     def clear(index, carry):
@@ -539,26 +584,23 @@
     vmem = pl.BlockSpec(memory_space=pltpu.VMEM)
     params = pltpu.CompilerParams(vmem_limit_bytes=48 * 1024 * 1024)
     block = (tok_count, block_size)
-    right_source, tiles = pl.pallas_call(
+    right_source, partial_rows = pl.pallas_call(
         functools.partial(forward_kernel, scale=scale_factor),
         out_shape=(
             jax.ShapeDtypeStruct((2 * column_blocks,) + block, jnp.bfloat16),
-            jax.ShapeDtypeStruct((slot_total, block_size, block_size), jnp.bfloat16),
+            jax.ShapeDtypeStruct((row_blocks,) + block, jnp.bfloat16),
         ),
-        in_specs=[smem] * 3 + [vmem] * 2,
+        in_specs=[smem] * 5 + [vmem] * 2,
         out_specs=(vmem, vmem),
-        scratch_shapes=[pltpu.VMEM((2 * column_blocks + 1,) + block, jnp.float32)],
+        scratch_shapes=[
+            pltpu.VMEM((2 * column_blocks + 1,) + block, jnp.float32),
+            pltpu.VMEM((row_blocks + 1,) + block, jnp.float32),
+        ],
         compiler_params=params,
-    )(left_at, right_at, sum_at, packed, left_source)
-    partial_rows = pl.pallas_call(
-        functools.partial(input_grad_kernel, scale=scale_factor),
-        out_shape=jax.ShapeDtypeStruct((row_blocks,) + block, jnp.bfloat16),
-        in_specs=[smem] * 3 + [vmem] * 2,
-        out_specs=vmem,
-        scratch_shapes=[pltpu.VMEM((row_blocks + 1,) + block, jnp.float32)],
-        compiler_params=params,
-    )(right_at, row_at, up_steps, packed, right_source)
-    block_grads, summed_rows = reduce_all(tiles, partial_rows)
+    )(left_at, right_at, sum_at, row_at, up_steps, packed, left_source)
+    block_grads, summed_rows = reduce_all(
+        left_at, right_at, left_source, right_source, partial_rows, scale_factor
+    )
     input_grad = (
         summed_rows.transpose(1, 0, 2).reshape(tok_count, tokens.shape[1]).astype(jnp.bfloat16)
     )

time: 188 us -> 170 us (0.904)
  Pallas kernels: 157 us -> 138 us
    pallas_call x2 -> x1, Pallas kernels: 65.7 us -> 55 us  [reduce_all(): pl.pallas_call(functools.partial(reduce_kernel, sizes, chunk_counts, scal...]
    pallas_call x1, Pallas kernels: 33.1 us -> 25.3 us  [per_device(): pl.pallas_call(functools.partial(forward_kernel, scale=scale_factor), out...]
    unnamed x14 -> x6, local copies, waits for them, and re-layouts: 5.85 us -> 5.51 us
where the time goes in v3:
time: 170 us; the launch traced here: 169 us
  Pallas kernels  138 us (81%)
  other arithmetic  21.4 us (13%)
  local copies, waits for them, and re-layouts  6.69 us (4%)
  between operations  2.06 us (1%)
    pallas_call x1, Pallas kernels, gather_all(): pl.pallas_call(functools.partial(gather_kernel, sizes, chunk_counts), out...  58.1 us
    pallas_call x1, Pallas kernels, reduce_all(): pl.pallas_call(functools.partial(reduce_kernel, sizes, chunk_counts, scal...  55 us
    pallas_call x1, Pallas kernels, per_device(): pl.pallas_call(functools.partial(forward_kernel, scale=scale_factor), out...  25.3 us
    select_n x1, other arithmetic, adam_step(): jnp.where(keep_slot, new_second, second_in)  11.6 us
    unnamed x6, local copies, waits for them, and re-layouts  5.51 us

profile of v3, /device:TPU:0, one launch (start us, length us, event | category | flops | bytes accessed | tf_op | source)
XLA Modules:
  0.0 168.6 jit_solution(13587100768665536794)
XLA Ops:
  1.3 1.3 slice_reduce_fusion.1
  3.3 1.4 reduce_sum.46
  4.7 0.7 add_compare_fusion
  5.3 0.7 broadcast_compare_fusion
  6.0 0.1 copy.24
  6.1 0.1 eq.45
  6.2 0.8 copy.31
  7.0 0.1 broadcast_in_dim.83
  7.1 0.8 copy.29
  7.9 0.1 broadcast_in_dim.77
  8.0 0.8 copy.23
  8.8 0.1 reshape.76
  8.9 0.3 reduce-window.9
  9.2 0.1 slice.13
  9.3 0.1 slice_reduce_fusion
  9.4 0.1 add_bitcast_fusion
  9.5 1.3 select_reduce_fusion
  10.8 0.1 power_subtract_fusion.1
  10.9 0.7 and_select_fusion
  11.6 0.7 broadcast_select_fusion
  12.2 1.1 copy.25
  13.4 0.2 copy.27
  13.6 1.1 copy.26
  14.7 0.2 copy.28
  14.9 2.6 %convert_element_type.9.own_packed = bf16[64,128,128]{2,1,0:T(8,128)(2,1)S(1)} convert(f32[64,128,128]{2,1,0:T(8,128)} %param.11) | non-fusion elementwise | flops 1048576 | bytes 6291456 | tf_op jit(solution)/shard_map/convert_element_type | solution.py:567
  17.5 58.1 %shard_map.120 = (bf16[256,128,128]{2,1,0:T(8,128)(2,1)}, bf16[128,128,128]{2,1,0:T(8,128)(2,1)}) custom-call(bf16[64,128,128]{2,1,0:T(8,128)(2,1)S(1)} %convert_element_type.9.own_packed, bf16[16,128,128]{2,1,0:T(8,128)(2,1)S(1)} %maximum_bitcast_fusion.own_left), custom_call_target="tpu_custom_call" | custom-call | tf_op jit(solution)/shard_map/pallas_call | solution.py:246
  75.6 25.3 %shard_map.121 = (bf16[32,128,128]{2,1,0:T(8,128)(2,1)S(1)}, bf16[64,128,128]{2,1,0:T(8,128)(2,1)S(1)}) custom-call(s32[256]{0:T(256)S(1)} %get-tuple-element.39.left_at, s32[256]{0:T(256)S(1)} %get-tuple-element.35.right_at, s32[256]{0:T(256)S(1)} %get-tuple-element.34.sum_at, s32[256]{0:T(256)S(1)} %get-tuple-element.31.row_at, s32[1]{0:T(128)} %bitcast.4.up_steps, ...), custom_call_target="tpu_custom_call" | custom-call | tf_op jit(solution)/shard_map/pallas_call | solution.py:587
  100.9 55.0 %shard_map.122 = (f32[64,128,128]{2,1,0:T(8,128)}, bf16[8,128,128]{2,1,0:T(8,128)(2,1)S(1)}) custom-call(s32[256]{0:T(256)S(1)} %get-tuple-element.39.left_at, s32[256]{0:T(256)S(1)} %get-tuple-element.35.right_at, bf16[128,128,128]{2,1,0:T(8,128)(2,1)} %get-tuple-element.10.left_ref, bf16[32,128,128]{2,1,0:T(8,128)(2,1)S(1)} %get-tuple-element.12.right_ref, ...), custom_call_target="tpu_custom_call" | custom-call | tf_op jit(solution)/shard_map/pallas_call | solution.py:434
  156.0 0.2 copy.30
  156.2 0.9 copy.32
  157.0 11.6 %fusion.2 = (f32[64,128,128]{2,1,0:T(8,128)}, f32[64,128,128]{2,1,0:T(8,128)}, f32[64,128,128]{2,1,0:T(8,128)}) fusion(f32[64,128,128]{2,1,0:T(8,128)} %param.13, f32[64,128,128]{2,1,0:T(8,128)} %get-tuple-element.15, f32[64]{0:T(128)S(1)} %convert_power_fusion, pred[64]{0:T(512)(128)(4,1)S(1)} %get-tuple-element.30, pred[64]{0:T(512)(128)(4,1)S(1)} %add_compare_fusion, ...), kind=kLoop, calls=%fused_computation.5 | loop fusion | flops 24117248 | bytes 29361280 | tf_op jit(solution)/shard_map/jit(_where)/select_n | solution.py:74
  (4 shorter events, 0.1 us)

commit v4 on v3

--- a/solution.py
+++ b/solution.py
@@ -24,25 +24,22 @@
 
 
 def slot_table(mask_grid, regrown_grid, last_grid, slot_total):
-    flags = mask_grid.reshape(-1)
+    codes = lax.optimization_barrier((mask_grid + 2 * regrown_grid + 4 * last_grid).reshape(-1))
+    flags = codes & 1
     numbered = jnp.cumsum(flags, dtype=jnp.int32) - 1
     block_total = flags.shape[0]
-    matches = (numbered[None, :] == jnp.arange(slot_total, dtype=jnp.int32)[:, None]) & (
-        flags[None, :] == 1
-    )
-    block_index = jnp.sum(
-        jnp.where(matches, jnp.arange(block_total, dtype=jnp.int32)[None, :], 0),
-        axis=1,
-        dtype=jnp.int32,
-    )
-    slot_regrown = jnp.sum(
-        jnp.where(matches, regrown_grid.reshape(-1)[None, :], 0), axis=1, dtype=jnp.int32
-    )
-    slot_last = jnp.sum(
-        jnp.where(matches, last_grid.reshape(-1)[None, :], 0), axis=1, dtype=jnp.int32
-    )
+    wanted = jnp.where(flags == 1, numbered, -1)
+    entries = jnp.arange(block_total, dtype=jnp.int32) + block_total * (codes >> 1)
+    matches = wanted[None, :] == jnp.arange(slot_total, dtype=jnp.int32)[:, None]
+    found = lax.optimization_barrier(
+        jnp.sum(jnp.where(matches, entries[None, :], 0), axis=1, dtype=jnp.int32)
+    )
+    block_index = found % block_total
+    slot_regrown = found // block_total & 1
+    slot_last = found // block_total // 2
     live_count = jnp.sum(flags, dtype=jnp.int32)
-    return (numbered, block_index, slot_regrown, slot_last, live_count)
+    up_count = jnp.sum(flags[: block_total // 2], dtype=jnp.int32)
+    return (block_index, slot_regrown, slot_last, live_count, up_count)
 
 
 def adam_step(
@@ -94,7 +91,7 @@
     )
 
 
-def greet(targets):
+def greet(targets, meanwhile=None):
     barrier = pltpu.get_barrier_semaphore()
     for axis, target, exists in targets:
 
@@ -104,6 +101,8 @@
                 barrier, inc=1, device_id={axis: target}, device_id_type=pl.DeviceIdType.MESH
             )
 
+    if meanwhile is not None:
+        meanwhile()
     pl.semaphore_wait(barrier, sum(jnp.where(exists, 1, 0) for _, _, exists in targets))
 
 
@@ -207,12 +206,37 @@
         self.own_copy().wait()
 
 
-def gather_kernel(sizes, chunk_counts, own_packed, own_left, packed_out, left_out, *sems):
+def gather_kernel(
+    sizes,
+    chunk_counts,
+    weights,
+    tokens,
+    grad_out,
+    packed_out,
+    left_out,
+    own_packed,
+    own_left,
+    *sems,
+):
     lines = [
         LineGather("dp", sizes[0], chunk_counts[0], own_packed, packed_out, sems[:5]),
         LineGather("tensor", sizes[1], chunk_counts[1], own_left, left_out, sems[5:]),
     ]
-    greet(lines[0].targets() + lines[1].targets())
+
+    def round_own():
+        side = own_left.shape[2]
+        local_rows = own_left.shape[0] // 2
+        for row in range(local_rows):
+            own_left[row] = tokens[:, row * side : (row + 1) * side]
+            own_left[local_rows + row] = grad_out[:, row * side : (row + 1) * side]
+
+        def round_block(index, carry):
+            own_packed[index] = weights[index].astype(jnp.bfloat16)
+            return carry
+
+        lax.fori_loop(0, own_packed.shape[0], round_block, 0)
+
+    greet(lines[0].targets() + lines[1].targets(), round_own)
     events = []
     for line in lines:
         for chunk in range(line.chunks):
@@ -239,23 +263,31 @@
     return [dma((size * chunks,))] + [dma((outer * chunks,))] * 3 + [dma]
 
 
-def gather_all(own_packed, own_left):
+def gather_all(weights, tokens, grad_out):
     sizes = (lax.axis_size("dp"), lax.axis_size("tensor"))
-    chunk_counts = (math.gcd(4, own_packed.shape[0]), math.gcd(2, own_left.shape[0]))
+    side = weights.shape[1]
+    own_left = (2 * tokens.shape[1] // side, tokens.shape[0], side)
+    chunk_counts = (math.gcd(4, weights.shape[0]), math.gcd(2, own_left[0]))
     vmem = pl.BlockSpec(memory_space=pltpu.VMEM)
+    anywhere = pl.BlockSpec(memory_space=pl.ANY)
     return pl.pallas_call(
         functools.partial(gather_kernel, sizes, chunk_counts),
         out_shape=(
-            jax.ShapeDtypeStruct((sizes[0] * own_packed.shape[0],) + own_packed.shape[1:], jnp.bfloat16),
-            jax.ShapeDtypeStruct((sizes[1] * own_left.shape[0],) + own_left.shape[1:], jnp.bfloat16),
+            jax.ShapeDtypeStruct((sizes[0] * weights.shape[0], side, side), jnp.bfloat16),
+            jax.ShapeDtypeStruct((sizes[1] * own_left[0],) + own_left[1:], jnp.bfloat16),
         ),
-        in_specs=[vmem, vmem],
-        out_specs=(pl.BlockSpec(memory_space=pl.ANY), pl.BlockSpec(memory_space=pl.ANY)),
-        scratch_shapes=line_sems(sizes[0], chunk_counts[0]) + line_sems(sizes[1], chunk_counts[1]),
+        in_specs=[vmem, vmem, vmem],
+        out_specs=(anywhere, anywhere),
+        scratch_shapes=[
+            pltpu.VMEM(weights.shape, jnp.bfloat16),
+            pltpu.VMEM(own_left, jnp.bfloat16),
+        ]
+        + line_sems(sizes[0], chunk_counts[0])
+        + line_sems(sizes[1], chunk_counts[1]),
         compiler_params=pltpu.CompilerParams(
             collective_id=0, has_side_effects=True, vmem_limit_bytes=48 * 1024 * 1024
         ),
-    )(own_packed, own_left)
+    )(weights, tokens, grad_out)
 
 
 class PairReduce:
@@ -448,7 +480,7 @@
     )(left_at, right_at, left_source, right_source, partial_rows)
 
 
-UNROLL = 4
+UNROLL = 8
 
 
 def forward_kernel(
@@ -557,16 +589,8 @@
     groups = lax.axis_size("dp")
     slot_total = owned_slots * groups
     step_value = step_now[0]
-    own_left = jnp.concatenate(
-        [
-            tokens.reshape(tok_count, local_rows, block_size),
-            grad_out.reshape(tok_count, local_rows, block_size),
-        ],
-        axis=1,
-    ).transpose(1, 0, 2)
-    own_packed = packed_weight_blocks.astype(jnp.bfloat16)
-    packed, left_source = gather_all(own_packed, own_left)
-    _, block_index, slot_regrown, slot_last, live_count = slot_table(
+    packed, left_source = gather_all(packed_weight_blocks, tokens, grad_out)
+    block_index, slot_regrown, slot_last, live_count, up_count = slot_table(
         block_mask, regrown, last_step, slot_total
     )
     matrix_of = block_index // (row_blocks * column_blocks)
@@ -578,7 +602,6 @@
     right_at = matrix_of * column_blocks + column_of
     sum_at = jnp.where(usable, right_at, 2 * column_blocks)
     row_at = jnp.where(usable & (matrix_of == 0), row_of, row_blocks)
-    up_count = jnp.sum(block_mask[0], dtype=jnp.int32)
     up_steps = ((up_count + UNROLL - 1) // UNROLL).reshape(1)
     smem = pl.BlockSpec(memory_space=pltpu.SMEM)
     vmem = pl.BlockSpec(memory_space=pltpu.VMEM)

time: 170 us -> 159 us (0.935)
  other arithmetic: 21.4 us -> 16.4 us
  Pallas kernels: 138 us -> 135 us
    pallas_call x1, Pallas kernels: 25.3 us -> 17.4 us  [per_device(): pl.pallas_call(functools.partial(forward_kernel, scale=scale_factor), out...]
    reduce_sum x3 -> x2, other arithmetic: 4 us -> 0.92 us  [the longest x1 0.63 us: slot_table(): up_count = jnp.sum(flags[:block_total // 2], dtype=jnp.int32)]
    pallas_call x1, Pallas kernels: 55 us -> 57.9 us  [reduce_all(): pl.pallas_call(functools.partial(reduce_kernel, sizes, chunk_counts, scal...]
    convert_element_type x1 -> x0, other arithmetic: 2.56 us -> none  [per_device(): own_packed = packed_weight_blocks.astype(jnp.bfloat16)]
    pallas_call x1, Pallas kernels: 58.1 us -> 59.9 us  [gather_all(): pl.pallas_call(functools.partial(gather_kernel, sizes, chunk_counts), out...]
    unnamed x6 -> x7, local copies, waits for them, and re-layouts: 5.51 us -> 4.76 us
where the time goes in v4:
time: 159 us
  Pallas kernels  135 us (85%)
  other arithmetic  16.4 us (10%)
  local copies, waits for them, and re-layouts  5.29 us (3%)
  between operations  2.04 us (1%)
    pallas_call x1, Pallas kernels, gather_all(): pl.pallas_call(functools.partial(gather_kernel, sizes, chunk_counts), out...  59.9 us
    pallas_call x1, Pallas kernels, reduce_all(): pl.pallas_call(functools.partial(reduce_kernel, sizes, chunk_counts, scal...  57.9 us
    pallas_call x1, Pallas kernels, per_device(): pl.pallas_call(functools.partial(forward_kernel, scale=scale_factor), out...  17.4 us
    select_n x1, other arithmetic, adam_step(): jnp.where(keep_slot, new_second, second_in)  11.6 us
    unnamed x7, local copies, waits for them, and re-layouts  4.76 us

profile of v4, /device:TPU:0, one launch (start us, length us, event | category | flops | bytes accessed | tf_op | source)
XLA Modules:
  0.0 158.9 jit_solution(14622920622522726230)
XLA Ops:
  1.3 0.8 multiply_add_fusion.1
  2.0 0.1 copy.16
  2.1 0.1 reshape.52
  2.2 0.3 reduce-window.9
  2.5 0.1 slice.13
  2.6 0.1 slice_reduce_fusion
  2.7 0.6 broadcast_and_fusion
  3.4 0.7 add_compare_fusion
  4.0 0.6 slice_reduce_fusion.1
  5.3 0.3 select_reduce_fusion
  5.6 0.7 and_select_fusion.1
  6.3 0.7 broadcast_select_fusion
  7.0 0.1 power_subtract_fusion.1
  7.1 0.0 copy-start.1
  7.1 0.9 copy-done.1
  8.1 0.0 copy-start.2
  8.1 0.9 copy-done.2
  9.0 59.9 %shard_map.120 = (bf16[256,128,128]{2,1,0:T(8,128)(2,1)}, bf16[128,128,128]{2,1,0:T(8,128)(2,1)S(1)}) custom-call(f32[64,128,128]{2,1,0:T(8,128)} %weights.1, bf16[128,1024]{1,0:T(8,128)(2,1)S(1)} %copy-done.1, bf16[128,1024]{1,0:T(8,128)(2,1)S(1)} %copy-done.2), custom_call_target="tpu_custom_call" | custom-call | tf_op jit(solution)/shard_map/pallas_call | solution.py:273
  68.9 0.0 copy-start
  68.9 2.0 %copy-done = bf16[128,128,128]{2,1,0:T(8,128)(2,1)} copy-done((bf16[128,128,128]{2,1,0:T(8,128)(2,1)}, bf16[128,128,128]{2,1,0:T(8,128)(2,1)S(1)}, u32[]{:S(2)}) %copy-start) | copy-done | bytes 4194328
  70.9 17.4 %shard_map.121 = (bf16[32,128,128]{2,1,0:T(8,128)(2,1)S(1)}, bf16[64,128,128]{2,1,0:T(8,128)(2,1)S(1)}) custom-call(s32[256]{0:T(256)S(1)} %get-tuple-element.44.left_at, s32[256]{0:T(256)S(1)} %get-tuple-element.35.right_at, s32[256]{0:T(256)S(1)} %get-tuple-element.34.sum_at, s32[256]{0:T(256)S(1)} %get-tuple-element.30.row_at, s32[1]{0:T(128)} %bitcast.2.up_steps, ...), custom_call_target="tpu_custom_call" | custom-call | tf_op jit(solution)/shard_map/pallas_call | solution.py:610
  88.3 57.9 %shard_map.122 = (f32[64,128,128]{2,1,0:T(8,128)}, bf16[8,128,128]{2,1,0:T(8,128)(2,1)S(1)}) custom-call(s32[256]{0:T(256)S(1)} %get-tuple-element.44.left_at, s32[256]{0:T(256)S(1)} %get-tuple-element.35.right_at, bf16[128,128,128]{2,1,0:T(8,128)(2,1)} %copy-done, bf16[32,128,128]{2,1,0:T(8,128)(2,1)S(1)} %get-tuple-element.12.right_ref, ...), custom_call_target="tpu_custom_call" | custom-call | tf_op jit(solution)/shard_map/pallas_call | solution.py:466
  146.3 0.2 copy.17
  146.4 0.9 copy.18
  147.3 11.6 %fusion.2 = (f32[64,128,128]{2,1,0:T(8,128)}, f32[64,128,128]{2,1,0:T(8,128)}, f32[64,128,128]{2,1,0:T(8,128)}) fusion(f32[64,128,128]{2,1,0:T(8,128)} %param.13, f32[64,128,128]{2,1,0:T(8,128)} %get-tuple-element.15, f32[64]{0:T(128)S(1)} %convert_power_fusion, pred[64]{0:T(512)(128)(4,1)S(1)} %get-tuple-element.27, pred[64]{0:T(512)(128)(4,1)S(1)} %add_compare_fusion, ...), kind=kLoop, calls=%fused_computation.5 | loop fusion | flops 24117248 | bytes 29361280 | tf_op jit(solution)/shard_map/jit(_where)/select_n | solution.py:71
  (5 shorter events, 0.1 us)
Async XLA Ops:
  7.1 1.0 copy-start.1
  8.1 0.9 copy-start.2
  68.9 2.0 %copy-start = (bf16[128,128,128]{2,1,0:T(8,128)(2,1)}, bf16[128,128,128]{2,1,0:T(8,128)(2,1)S(1)}, u32[]{:S(2)}) copy-start(bf16[128,128,128]{2,1,0:T(8,128)(2,1)S(1)} %get-tuple-element.10.left_ref) | copy-start | bytes 12582916

commit v5 on v4

--- a/solution.py
+++ b/solution.py
@@ -238,11 +238,12 @@
 
     greet(lines[0].targets() + lines[1].targets(), round_own)
     events = []
-    for line in lines:
+    for line, weight in zip(lines, (1.5, 1.0)):
         for chunk in range(line.chunks):
             events.append((chunk / line.chunks, line, 0, chunk))
             for distance in range(1, line.outer):
-                when = 1 + (distance - 1 + (chunk + 1) / line.chunks) / (line.outer - 1)
+                passed = (distance - 1 + (chunk + 1) / line.chunks) / (line.outer - 1)
+                when = 1 + weight * passed
                 events.append((when, line, distance, chunk))
     events.sort(key=lambda event: event[0])
     for when, line, distance, chunk in events:
@@ -267,7 +268,7 @@
     sizes = (lax.axis_size("dp"), lax.axis_size("tensor"))
     side = weights.shape[1]
     own_left = (2 * tokens.shape[1] // side, tokens.shape[0], side)
-    chunk_counts = (math.gcd(4, weights.shape[0]), math.gcd(2, own_left[0]))
+    chunk_counts = (math.gcd(8, weights.shape[0]), math.gcd(4, own_left[0]))
     vmem = pl.BlockSpec(memory_space=pltpu.VMEM)
     anywhere = pl.BlockSpec(memory_space=pl.ANY)
     return pl.pallas_call(
@@ -455,7 +456,7 @@
     side = left_source.shape[2]
     tile_shape = (left_at.shape[0], side, side)
     shards = (tile_shape[0] // sizes[0], partial_rows.shape[0] // sizes[1])
-    chunk_counts = (math.gcd(4, shards[0]), math.gcd(2, shards[1]))
+    chunk_counts = (math.gcd(8, shards[0]), math.gcd(2, shards[1]))
     vmem = pl.BlockSpec(memory_space=pltpu.VMEM)
     smem = pl.BlockSpec(memory_space=pltpu.SMEM)
     scratch = [pltpu.VMEM(tile_shape, jnp.bfloat16)]

time: 159 us -> 154 us (0.969)
  Pallas kernels: 135 us -> 130 us
    pallas_call x1, Pallas kernels: 59.9 us -> 55.2 us  [gather_all(): pl.pallas_call(functools.partial(gather_kernel, sizes, chunk_counts), out...]
where the time goes in v5:
time: 154 us
  Pallas kernels  130 us (84%)
  other arithmetic  16.4 us (11%)
  local copies, waits for them, and re-layouts  5.29 us (3%)
  between operations  2.04 us (1%)
    pallas_call x1, Pallas kernels, reduce_all(): pl.pallas_call(functools.partial(reduce_kernel, sizes, chunk_counts, scal...  57.7 us
    pallas_call x1, Pallas kernels, gather_all(): pl.pallas_call(functools.partial(gather_kernel, sizes, chunk_counts), out...  55.2 us
    pallas_call x1, Pallas kernels, per_device(): pl.pallas_call(functools.partial(forward_kernel, scale=scale_factor), out...  17.4 us
    select_n x1, other arithmetic, adam_step(): jnp.where(keep_slot, new_second, second_in)  11.6 us
    unnamed x7, local copies, waits for them, and re-layouts  4.76 us

profile of v5, /device:TPU:0, one launch (start us, length us, event | category | flops | bytes accessed | tf_op | source)
XLA Modules:
  0.0 154.1 jit_solution(8211407244393025527)
XLA Ops:
  1.3 0.8 multiply_add_fusion.1
  2.0 0.1 copy.16
  2.1 0.1 reshape.52
  2.2 0.3 reduce-window.9
  2.5 0.1 slice.13
  2.6 0.1 slice_reduce_fusion
  2.7 0.6 broadcast_and_fusion
  3.4 0.7 add_compare_fusion
  4.0 0.6 slice_reduce_fusion.1
  5.3 0.3 select_reduce_fusion
  5.6 0.7 and_select_fusion.1
  6.3 0.7 broadcast_select_fusion
  7.0 0.1 power_subtract_fusion.1
  7.1 0.0 copy-start.1
  7.1 0.9 copy-done.1
  8.1 0.0 copy-start.2
  8.1 0.9 copy-done.2
  9.0 55.2 %shard_map.120 = (bf16[256,128,128]{2,1,0:T(8,128)(2,1)}, bf16[128,128,128]{2,1,0:T(8,128)(2,1)S(1)}) custom-call(f32[64,128,128]{2,1,0:T(8,128)} %weights.1, bf16[128,1024]{1,0:T(8,128)(2,1)S(1)} %copy-done.1, bf16[128,1024]{1,0:T(8,128)(2,1)S(1)} %copy-done.2), custom_call_target="tpu_custom_call" | custom-call | tf_op jit(solution)/shard_map/pallas_call | solution.py:274
  64.3 0.0 copy-start
  64.3 2.0 %copy-done = bf16[128,128,128]{2,1,0:T(8,128)(2,1)} copy-done((bf16[128,128,128]{2,1,0:T(8,128)(2,1)}, bf16[128,128,128]{2,1,0:T(8,128)(2,1)S(1)}, u32[]{:S(2)}) %copy-start) | copy-done | bytes 4194328
  66.3 17.4 %shard_map.121 = (bf16[32,128,128]{2,1,0:T(8,128)(2,1)S(1)}, bf16[64,128,128]{2,1,0:T(8,128)(2,1)S(1)}) custom-call(s32[256]{0:T(256)S(1)} %get-tuple-element.44.left_at, s32[256]{0:T(256)S(1)} %get-tuple-element.35.right_at, s32[256]{0:T(256)S(1)} %get-tuple-element.34.sum_at, s32[256]{0:T(256)S(1)} %get-tuple-element.30.row_at, s32[1]{0:T(128)} %bitcast.2.up_steps, ...), custom_call_target="tpu_custom_call" | custom-call | tf_op jit(solution)/shard_map/pallas_call | solution.py:611
  83.7 57.7 %shard_map.122 = (f32[64,128,128]{2,1,0:T(8,128)}, bf16[8,128,128]{2,1,0:T(8,128)(2,1)S(1)}) custom-call(s32[256]{0:T(256)S(1)} %get-tuple-element.44.left_at, s32[256]{0:T(256)S(1)} %get-tuple-element.35.right_at, bf16[128,128,128]{2,1,0:T(8,128)(2,1)} %copy-done, bf16[32,128,128]{2,1,0:T(8,128)(2,1)S(1)} %get-tuple-element.12.right_ref, ...), custom_call_target="tpu_custom_call" | custom-call | tf_op jit(solution)/shard_map/pallas_call | solution.py:467
  141.5 0.2 copy.17
  141.6 0.9 copy.18
  142.5 11.6 %fusion.2 = (f32[64,128,128]{2,1,0:T(8,128)}, f32[64,128,128]{2,1,0:T(8,128)}, f32[64,128,128]{2,1,0:T(8,128)}) fusion(f32[64,128,128]{2,1,0:T(8,128)} %param.13, f32[64,128,128]{2,1,0:T(8,128)} %get-tuple-element.15, f32[64]{0:T(128)S(1)} %convert_power_fusion, pred[64]{0:T(512)(128)(4,1)S(1)} %get-tuple-element.27, pred[64]{0:T(512)(128)(4,1)S(1)} %add_compare_fusion, ...), kind=kLoop, calls=%fused_computation.5 | loop fusion | flops 24117248 | bytes 29361280 | tf_op jit(solution)/shard_map/jit(_where)/select_n | solution.py:71
  (5 shorter events, 0.1 us)
Async XLA Ops:
  7.1 1.0 copy-start.1
  8.1 0.9 copy-start.2
  64.3 2.0 %copy-start = (bf16[128,128,128]{2,1,0:T(8,128)(2,1)}, bf16[128,128,128]{2,1,0:T(8,128)(2,1)S(1)}, u32[]{:S(2)}) copy-start(bf16[128,128,128]{2,1,0:T(8,128)(2,1)S(1)} %get-tuple-element.10.left_ref) | copy-start | bytes 12582916
